TPU v7x, 128 devices: a whole 4x4x4 slice. The times are simulated.
128 devices in a mesh: edge: 64 (over x, z, y), rep: 2 (over core).
Axes of the slice: x: 4, y: 4, z: 4, core: 2. Of those that a mesh axis runs over, the one named last changes fastest.
Arguments:
- edge_feats: bfloat16 [262144, 512], P(('rep', 'edge')), parts along dimension 0, may hold values from -6 to 6
- atom_feats: bfloat16 [32768, 512], P(('rep', 'edge')), parts along dimension 0, may hold values from -6 to 6
- w_edge: bfloat16 [6, 512, 512], replicated, may hold values from -0.25 to 0.25
- w_atom: bfloat16 [2, 512, 512], replicated, may hold values from -0.25 to 0.25
- send_order: int32 [128, 2048], P(('rep', 'edge')), parts along dimension 0, may hold values from 0 to 2047, as said below
- recv_pos: int32 [128, 2048], P(('rep', 'edge')), parts along dimension 0, may hold values from 0 to 2047, as said below
- edge_list: int32 [128, 2048], P(('rep', 'edge')), parts along dimension 0, may hold values from 0 to 31, never falling along the last dimension, each value on 1 to 192 neighbouring positions
- edge_atom: int32 [128, 2048], P(('rep', 'edge')), parts along dimension 0, may hold values from 0 to 127
- list_block: int32 [128, 32], P(('rep', 'edge')), parts along dimension 0, may hold values from 0 to 127, as said below
- block_home: int32 [256], P('rep'), parts along dimension 0, may hold values from 0 to 127, as said below
Outputs:
- edge_out: bfloat16 [262144, 512], P(('rep', 'edge')), parts along dimension 0
- atom_out: bfloat16 [32768, 512], P(('rep', 'edge')), parts along dimension 0
There are 2 independent parts, one for each index of `rep`. A program takes and returns all parts, laid end to end along the dimension named above; an argument that names none is the same for every part. Nothing has to cross between parts.
Inputs may be any that keep to these rules, and one draw needn't show every extreme that they name: Each row of send_order is a permutation of the device's rows; each row of recv_pos is a permutation of the places. Every edge has exactly 32 reverse partners' messages passing between its device and each device, the pairing is symmetric, and no edge is its own partner. `recv_pos`: together with send_order the pairing of every edge with its reverse edge as described there. `list_block`: the 32 lists of one device aim at atom blocks stored on 32 different devices. `block_home`: A permutation of the block ids' storage positions.
All inputs are finite; a program needn't handle non-finite values.
Results may differ from a plain program's by a relative error of at most 0.0095.
Values may be sent and summed in bfloat16 or wider, within the bound.
A program may use at most 128 MiB of HBM per device.

v0:
```python
import jax
import jax.numpy as jnp
from jax import lax
from jax.sharding import PartitionSpec as P

ABLK = 128
BLOCKS = 2
AB_DEV = 2


def dense_silu(values, weight):
    return jax.nn.silu(jnp.dot(values, weight, preferred_element_type=jnp.float32)).astype(
        jnp.bfloat16
    )


def list_sums(third, edge_lists, edge_slots, list_count):
    row_count, feat = third.shape
    window_len = 3 * row_count // list_count
    list_table = jnp.arange(list_count, dtype=jnp.int32)
    offsets = jnp.sum((edge_lists[:, None] < list_table[None, :]).astype(jnp.int32), axis=0)
    window = offsets[:, None] + jnp.arange(window_len, dtype=jnp.int32)[None, :]
    padded_rows = jnp.concatenate([third, jnp.zeros((window_len, feat), third.dtype)], axis=0)
    padded_lists = jnp.concatenate([edge_lists, jnp.full((window_len,), -1, jnp.int32)], axis=0)
    padded_slots = jnp.concatenate([edge_slots, jnp.zeros((window_len,), jnp.int32)], axis=0)
    window_rows = jnp.take(padded_rows, window, axis=0)
    window_lists = jnp.take(padded_lists, window, axis=0)
    window_slots = jnp.take(padded_slots, window, axis=0)
    atom_table = jnp.arange(ABLK, dtype=jnp.int32)
    onehot = (
        (window_slots[:, None, :] == atom_table[None, :, None])
        & (window_lists[:, None, :] == list_table[:, None, None])
    ).astype(jnp.bfloat16)
    sums = jnp.einsum("lam,lmh->lah", onehot, window_rows, preferred_element_type=jnp.float32)
    return sums.reshape(list_count * ABLK, feat)


def on_device(
    edge_feats,
    atom_feats,
    w_edge,
    w_atom,
    send_order,
    recv_pos,
    edge_list,
    edge_atom,
    list_block,
    block_home,
):
    peer_count = lax.axis_size("edge")
    row_count, feat = edge_feats.shape
    list_count = list_block.shape[1]
    block_count = block_home.shape[0]
    row_order = send_order[0]
    recv_rows = recv_pos[0]
    edge_lists = edge_list[0]
    edge_slots = edge_atom[0]
    list_blocks = list_block[0]
    block_table = jnp.arange(block_count, dtype=jnp.int32)
    list_place = jnp.sum(
        jnp.where(list_blocks[:, None] == block_table[None, :], block_home[None, :], 0), axis=1
    )
    list_owner = list_place // AB_DEV
    list_table = jnp.arange(list_count, dtype=jnp.int32)
    in_list = edge_lists[:, None] == list_table[None, :]
    edge_owner = jnp.sum(jnp.where(in_list, list_owner[None, :], 0), axis=1)
    peer_table = jnp.arange(peer_count, dtype=jnp.int32)
    placing = list_owner[None, :] == peer_table[:, None]
    place_matrix = placing.astype(jnp.bfloat16)
    send_ids = jnp.max(jnp.where(placing, list_blocks[None, :], -1), axis=1)
    message = edge_feats
    atoms = atom_feats
    for layer_block in range(BLOCKS):
        first = dense_silu(message, w_edge[3 * layer_block])
        second = dense_silu(first, w_edge[3 * layer_block + 1])
        outgoing = jnp.take(second, row_order, axis=0)
        arrived = lax.all_to_all(outgoing, "edge", split_axis=0, concat_axis=0, tiled=True)
        reverse = jnp.take(arrived, recv_rows, axis=0)
        paired = (second.astype(jnp.float32) + reverse.astype(jnp.float32)).astype(jnp.bfloat16)
        third = dense_silu(paired, w_edge[3 * layer_block + 2])
        partial_value = list_sums(third, edge_lists, edge_slots, list_count).astype(jnp.bfloat16)
        send_vals = jnp.dot(
            place_matrix,
            partial_value.reshape(list_count, ABLK * feat),
            preferred_element_type=jnp.float32,
        )
        send_vals = send_vals.astype(jnp.bfloat16).reshape(peer_count, ABLK, feat)
        recv_vals, recv_ids = (
            lax.all_to_all(send_vals, "edge", split_axis=0, concat_axis=0, tiled=True),
            lax.all_to_all(send_ids, "edge", split_axis=0, concat_axis=0, tiled=True),
        )
        valid = recv_ids >= 0
        safe_ids = jnp.where(valid, recv_ids, 0)
        recv_place = jnp.sum(
            jnp.where(safe_ids[:, None] == block_table[None, :], block_home[None, :], 0), axis=1
        )
        local_slot = recv_place % AB_DEV
        slot_table = jnp.arange(AB_DEV, dtype=jnp.int32)
        collect = ((local_slot[None, :] == slot_table[:, None]) & valid[None, :]).astype(
            jnp.bfloat16
        )
        gathered = jnp.dot(
            collect, recv_vals.reshape(peer_count, ABLK * feat), preferred_element_type=jnp.float32
        )
        gathered = gathered.reshape(AB_DEV * ABLK, feat).astype(jnp.bfloat16)
        update = jax.nn.silu(
            jnp.dot(gathered, w_atom[layer_block], preferred_element_type=jnp.float32)
        )
        atoms = (atoms.astype(jnp.float32) + update).astype(jnp.bfloat16)
        back = jnp.dot(
            collect.T, atoms.reshape(AB_DEV, ABLK * feat), preferred_element_type=jnp.float32
        )
        back = back.astype(jnp.bfloat16).reshape(peer_count, ABLK, feat)
        home_rows = lax.all_to_all(back, "edge", split_axis=0, concat_axis=0, tiled=True)
        fetched = jnp.take(
            home_rows.reshape(peer_count * ABLK, feat), edge_owner * ABLK + edge_slots, axis=0
        )
        message = (
            message.astype(jnp.float32) + third.astype(jnp.float32) + fetched.astype(jnp.float32)
        ).astype(jnp.bfloat16)
    return (message, atoms)


def solution(mesh):
    placed = (
        P(("rep", "edge"), None),
        P(("rep", "edge"), None),
        P(),
        P(),
        P(("rep", "edge"), None),
        P(("rep", "edge"), None),
        P(("rep", "edge"), None),
        P(("rep", "edge"), None),
        P(("rep", "edge"), None),
        P("rep"),
    )
    return jax.shard_map(
        on_device,
        mesh=mesh,
        in_specs=placed,
        out_specs=(P(("rep", "edge"), None), P(("rep", "edge"), None)),
        check_vma=False,
    )
```

profile of v0, /device:TPU:1, one launch (start us, length us, event | category | flops | bytes accessed | tf_op | source)
XLA Modules:
  0.0 865.2 jit_solution(18121740486668706501)
XLA Ops:
  0.6 0.7 compare_and_fusion.3
  1.3 0.7 fusion.71
  2.0 5.1 multiply_convert_fusion.4
  7.2 9.2 %gather_fusion = bf16[2048,512]{1,0:T(8,128)(2,1)} fusion(bf16[2048,512]{1,0:T(8,128)(2,1)S(1)} %multiply_convert_fusion.4, s32[2048]{0:T(1024)S(1)} %fusion.71), kind=kCustom, calls=%fused_computation.clone | custom fusion | bytes 4202496 | tf_op jit(solution)/shard_map/jit(_take)/gather | solution.py:76
  16.4 2.8 broadcast_select_fusion.1
  19.2 12.0 %all-to-all-start = ((bf16[64,32,512]{2,1,0:T(8,128)(2,1)}), bf16[64,32,512]{2,1,0:T(8,128)(2,1)S(1)}, u32[]{:S(2)}, u32[]{:S(2)}) async-start(bf16[64,32,512]{2,1,0:T(8,128)(2,1)} %bitcast.95), calls=%async_computation | async-start | bytes 4194304 | tf_op jit(solution)/shard_map/all_to_all | solution.py:77
  31.2 0.2 select_reduce_fusion.3
  31.4 0.1 select_reduce_fusion.2
  31.5 0.7 copy.14
  32.2 0.1 select_reduce_fusion
  32.4 0.1 compare_select_fusion
  32.5 0.1 reshape.232
  32.6 34.3 %gather_fusion.3 = s32[6144]{0:T(1024)S(1)} fusion(s32[2240]{0:T(1024)S(1)} %concatenate.15, s32[6144]{0:T(1024)S(1)} %broadcast_clamp_fusion), kind=kCustom, calls=%fused_computation.7.clone | custom fusion | bytes 73728 | tf_op jit(solution)/shard_map/jit(_take)/gather | solution.py:27
  67.0 34.3 %gather_fusion.2 = s32[6144]{0:T(1024)S(1)} fusion(s32[2240]{0:T(1024)S(1)} %concatenate.14, s32[6144]{0:T(1024)S(1)} %broadcast_clamp_fusion), kind=kCustom, calls=%fused_computation.1.clone | custom fusion | bytes 73728 | tf_op jit(solution)/shard_map/jit(_take)/gather | solution.py:28
  101.3 0.1 select_compare_fusion
  101.4 0.1 broadcast_select_fusion.2
  101.5 10.0 %all-to-all-start.1 = ((s32[64,1,1]{2,1,0:T(1,128)}), s32[64,1,1]{2,1,0:T(1,128)S(1)}, u32[]{:S(2)}, u32[]{:S(2)}) async-start(s32[64,1,1]{2,1,0:T(1,128)} %copy.14), calls=%async_computation.1 | async-start | bytes 65536 | tf_op jit(solution)/shard_map/all_to_all | solution.py:90
  111.5 9.2 %gather_fusion.1 = bf16[2048,512]{1,0:T(8,128)(2,1)} fusion(bf16[2048,512]{1,0:T(8,128)(2,1)S(1)} %bitcast.79, s32[2048]{0:T(1024)S(1)} %fusion.72), kind=kCustom, calls=%fused_computation.4.clone | custom fusion | bytes 4202496 | tf_op jit(solution)/shard_map/jit(_take)/gather | solution.py:78
  120.7 4.2 multiply_convert_fusion.3
  124.9 1.3 copy-done.3
  126.2 0.1 concatenate.16
  126.4 25.5 %gather_fusion.4 = bf16[6144,512]{1,0:T(8,128)(2,1)} fusion(bf16[2240,512]{1,0:T(8,128)(2,1)S(1)} %concatenate.16, s32[6144]{0:T(1024)S(1)} %broadcast_clamp_fusion), kind=kCustom, calls=%fused_computation.2.clone | custom fusion | bytes 12607488 | tf_op jit(solution)/shard_map/jit(_take)/gather | solution.py:26
  151.9 6.4 fusion.11
  158.3 2.4 copy.15
  160.7 5.7 convolution_convert_fusion.3
  166.4 9.9 %copy.16 = bf16[8,8,128,512]{3,2,1,0:T(8,128)(2,1)} copy(bf16[8,8,128,512]{3,1,2,0:T(8,128)(2,1)} %bitcast.86) | data formatting | bytes 16777216
  176.3 10.4 %all-to-all-start.2 = ((bf16[64,128,512]{2,1,0:T(8,128)(2,1)}), bf16[64,128,512]{2,1,0:T(8,128)(2,1)}, u32[]{:S(2)}, u32[]{:S(2)}) async-start(bf16[64,128,512]{2,1,0:T(8,128)(2,1)} %bitcast.82), calls=%async_computation.2 | async-start | bytes 16777216 | tf_op jit(solution)/shard_map/all_to_all | solution.py:89
  186.7 1.2 reduce
  187.9 0.2 select_reduce_fusion.1
  188.1 103.8 %all-to-all-done.2 = bf16[64,128,512]{2,1,0:T(8,128)(2,1)} async-done(((bf16[64,128,512]{2,1,0:T(8,128)(2,1)}), bf16[64,128,512]{2,1,0:T(8,128)(2,1)}, u32[]{:S(2)}, u32[]{:S(2)}) %all-to-all-start.2) | async-done | bytes 8388640 | tf_op jit(solution)/shard_map/all_to_all | solution.py:89
  292.0 11.8 %copy.17 = bf16[8,8,128,512]{3,1,2,0:T(8,128)(2,1)} copy(bf16[8,8,128,512]{3,2,1,0:T(8,128)(2,1)} %bitcast.26) | data formatting | bytes 16777216
  303.7 4.7 convolution_convert_fusion.5
  308.4 0.2 convert_element_type.133
  308.6 0.4 add_convert_fusion.11
  309.0 0.2 reshape.126
  309.2 5.6 convolution_convert_fusion.2
  314.8 10.3 %copy.18 = bf16[8,8,128,512]{3,2,1,0:T(8,128)(2,1)} copy(bf16[8,8,128,512]{3,1,2,0:T(8,128)(2,1)} %bitcast.88) | data formatting | bytes 16777216
  325.1 23.0 %all-to-all-start.3 = ((bf16[64,128,512]{2,1,0:T(8,128)(2,1)}), bf16[64,128,512]{2,1,0:T(8,128)(2,1)}, u32[]{:S(2)}, u32[]{:S(2)}) async-start(bf16[64,128,512]{2,1,0:T(8,128)(2,1)} %bitcast.83), calls=%async_computation.3 | async-start | bytes 16777216 | tf_op jit(solution)/shard_map/all_to_all | solution.py:114
  348.2 109.8 %all-to-all-done.3 = bf16[64,128,512]{2,1,0:T(8,128)(2,1)} async-done(((bf16[64,128,512]{2,1,0:T(8,128)(2,1)}), bf16[64,128,512]{2,1,0:T(8,128)(2,1)}, u32[]{:S(2)}, u32[]{:S(2)}) %all-to-all-start.3) | async-done | bytes 8388640 | tf_op jit(solution)/shard_map/all_to_all | solution.py:114
  458.0 13.7 %gather_fusion.5 = bf16[2048,512]{1,0:T(8,128)(2,1)} fusion(bf16[8192,512]{1,0:T(8,128)(2,1)} %bitcast.13, s32[2048]{0:T(1024)S(1)} %broadcast_clamp_fusion.1), kind=kCustom, calls=%fused_computation.3.clone | custom fusion | bytes 4202496 | tf_op jit(solution)/shard_map/jit(_take)/gather | solution.py:115
  471.7 6.2 multiply_convert_fusion.1
  478.0 9.2 %gather_fusion.6 = bf16[2048,512]{1,0:T(8,128)(2,1)} fusion(bf16[2048,512]{1,0:T(8,128)(2,1)S(1)} %multiply_convert_fusion.1, s32[2048]{0:T(1024)S(1)} %fusion.71), kind=kCustom, calls=%fused_computation.5.clone | custom fusion | bytes 4202496 | tf_op jit(solution)/shard_map/jit(_take)/gather | solution.py:76
  487.1 1.8 broadcast_select_fusion
  488.9 51.1 %all_to_all.57 = bf16[64,32,512]{2,1,0:T(8,128)(2,1)S(1)} all-to-all(bf16[64,32,512]{2,1,0:T(8,128)(2,1)S(1)} %bitcast.96), channel_id=1, replica_groups=mesh['edge'=64,'rep'=2] {'edge'}, dimensions={0} | all-to-all | bytes 4194304 | tf_op jit(solution)/shard_map/all_to_all | solution.py:77
  540.0 9.2 %gather_fusion.7 = bf16[2048,512]{1,0:T(8,128)(2,1)} fusion(bf16[2048,512]{1,0:T(8,128)(2,1)S(1)} %bitcast.80, s32[2048]{0:T(1024)S(1)} %fusion.72), kind=kCustom, calls=%fused_computation.6.clone | custom fusion | bytes 4202496 | tf_op jit(solution)/shard_map/jit(_take)/gather | solution.py:78
  549.2 4.2 multiply_convert_fusion
  553.4 1.3 copy-done.4
  554.7 0.1 concatenate.17
  554.9 25.5 %gather_fusion.8 = bf16[6144,512]{1,0:T(8,128)(2,1)} fusion(bf16[2240,512]{1,0:T(8,128)(2,1)S(1)} %concatenate.17, s32[6144]{0:T(1024)S(1)} %broadcast_clamp_fusion), kind=kCustom, calls=%fused_computation.8.clone | custom fusion | bytes 12607488 | tf_op jit(solution)/shard_map/jit(_take)/gather | solution.py:26
  580.4 6.4 fusion.16
  586.8 2.4 copy.19
  589.2 5.7 convolution_convert_fusion.1
  594.9 9.9 %copy.20 = bf16[8,8,128,512]{3,2,1,0:T(8,128)(2,1)} copy(bf16[8,8,128,512]{3,1,2,0:T(8,128)(2,1)} %bitcast.84) | data formatting | bytes 16777216
  604.8 107.2 %all_to_all.58 = bf16[64,128,512]{2,1,0:T(8,128)(2,1)} all-to-all(bf16[64,128,512]{2,1,0:T(8,128)(2,1)} %bitcast.89), channel_id=1, replica_groups=mesh['edge'=64,'rep'=2] {'edge'}, dimensions={0} | all-to-all | bytes 16777216 | tf_op jit(solution)/shard_map/all_to_all | solution.py:89
  712.0 11.8 %copy.21 = bf16[8,8,128,512]{3,1,2,0:T(8,128)(2,1)} copy(bf16[8,8,128,512]{3,2,1,0:T(8,128)(2,1)} %bitcast.90) | data formatting | bytes 16777216
  723.8 4.7 convolution_convert_fusion.4
  728.4 0.2 convert_element_type.151
  728.7 0.4 add_convert_fusion.10
  729.1 0.2 reshape.131
  729.2 5.6 convolution_convert_fusion
  734.9 10.1 %copy.22 = bf16[8,8,128,512]{3,2,1,0:T(8,128)(2,1)} copy(bf16[8,8,128,512]{3,1,2,0:T(8,128)(2,1)} %bitcast.85) | data formatting | bytes 16777216
  745.0 100.6 %all_to_all.59 = bf16[64,128,512]{2,1,0:T(8,128)(2,1)} all-to-all(bf16[64,128,512]{2,1,0:T(8,128)(2,1)} %bitcast.92), channel_id=1, replica_groups=mesh['edge'=64,'rep'=2] {'edge'}, dimensions={0} | all-to-all | bytes 16777216 | tf_op jit(solution)/shard_map/all_to_all | solution.py:114
  845.6 13.9 %gather_fusion.9 = bf16[2048,512]{1,0:T(8,128)(2,1)} fusion(bf16[8192,512]{1,0:T(8,128)(2,1)} %bitcast.81, s32[2048]{0:T(1024)S(1)} %broadcast_clamp_fusion.1), kind=kCustom, calls=%fused_computation.9.clone | custom fusion | bytes 4202496 | tf_op jit(solution)/shard_map/jit(_take)/gather | solution.py:115
  859.5 5.2 add_convert_fusion
  (42 shorter events, 0.3 us)
Async XLA Ops:
  7.2 9.2 %copy-start = (bf16[2048,512]{1,0:T(8,128)(2,1)}, bf16[2048,512]{1,0:T(8,128)(2,1)S(1)}, u32[]{:S(2)}) copy-start(bf16[2048,512]{1,0:T(8,128)(2,1)S(1)} %multiply_convert_fusion.4) | copy-start | bytes 6291460
  16.4 14.8 %copy-start.12 = (s32[1,32]{1,0:T(1,128)S(1)}, s32[1,32]{1,0:T(1,128)}, u32[]{:S(2)}) copy-start(s32[1,32]{1,0:T(1,128)} %param.26) | copy-start | bytes 388
  16.4 14.8 %copy-start.13 = (s32[128]{0:T(128)S(1)}, s32[128]{0:T(128)}, u32[]{:S(2)}) copy-start(s32[128]{0:T(128)} %param.27) | copy-start | bytes 1540
  16.4 15.8 %copy-start.8 = (s32[1,2048]{1,0:T(1,128)S(1)}, s32[1,2048]{1,0:T(1,128)}, u32[]{:S(2)}) copy-start(s32[1,2048]{1,0:T(1,128)} %param.24) | copy-start | bytes 24580
  19.2 82.3 %all-to-all-start = ((bf16[64,32,512]{2,1,0:T(8,128)(2,1)}), bf16[64,32,512]{2,1,0:T(8,128)(2,1)S(1)}, u32[]{:S(2)}, u32[]{:S(2)}) async-start(bf16[64,32,512]{2,1,0:T(8,128)(2,1)} %bitcast.95), calls=%async_computation | async-start | bytes 4194304 | tf_op jit(solution)/shard_map/all_to_all | solution.py:77
  32.6 34.4 %copy-start.6 = (s32[1,2048]{1,0:T(1,128)S(1)}, s32[1,2048]{1,0:T(1,128)}, u32[]{:S(2)}) copy-start(s32[1,2048]{1,0:T(1,128)} %param.25) | copy-start | bytes 24580
  66.9 34.4 %copy-start.7 = (s32[1,2048]{1,0:T(1,128)S(1)}, s32[1,2048]{1,0:T(1,128)}, u32[]{:S(2)}) copy-start(s32[1,2048]{1,0:T(1,128)} %param.23) | copy-start | bytes 24580
  101.5 74.8 %all-to-all-start.1 = ((s32[64,1,1]{2,1,0:T(1,128)}), s32[64,1,1]{2,1,0:T(1,128)S(1)}, u32[]{:S(2)}, u32[]{:S(2)}) async-start(s32[64,1,1]{2,1,0:T(1,128)} %copy.14), calls=%async_computation.1 | async-start | bytes 65536 | tf_op jit(solution)/shard_map/all_to_all | solution.py:90
  124.9 1.3 copy-start.3
  176.3 115.7 %all-to-all-start.2 = ((bf16[64,128,512]{2,1,0:T(8,128)(2,1)}), bf16[64,128,512]{2,1,0:T(8,128)(2,1)}, u32[]{:S(2)}, u32[]{:S(2)}) async-start(bf16[64,128,512]{2,1,0:T(8,128)(2,1)} %bitcast.82), calls=%async_computation.2 | async-start | bytes 16777216 | tf_op jit(solution)/shard_map/all_to_all | solution.py:89
  303.7 4.9 copy-start.9
  303.7 4.9 copy-start.11
  325.1 132.9 %all-to-all-start.3 = ((bf16[64,128,512]{2,1,0:T(8,128)(2,1)}), bf16[64,128,512]{2,1,0:T(8,128)(2,1)}, u32[]{:S(2)}, u32[]{:S(2)}) async-start(bf16[64,128,512]{2,1,0:T(8,128)(2,1)} %bitcast.83), calls=%async_computation.3 | async-start | bytes 16777216 | tf_op jit(solution)/shard_map/all_to_all | solution.py:114
  478.0 9.2 %copy-start.1 = (bf16[2048,512]{1,0:T(8,128)(2,1)}, bf16[2048,512]{1,0:T(8,128)(2,1)S(1)}, u32[]{:S(2)}) copy-start(bf16[2048,512]{1,0:T(8,128)(2,1)S(1)} %multiply_convert_fusion.1) | copy-start | bytes 6291460
  553.4 1.3 copy-start.4
  723.8 4.9 copy-start.10
  729.0 5.8 copy-start.5
  845.6 13.9 %copy-start.2 = (bf16[2048,512]{1,0:T(8,128)(2,1)S(1)}, bf16[2048,512]{1,0:T(8,128)(2,1)}, u32[]{:S(2)}) copy-start(bf16[2048,512]{1,0:T(8,128)(2,1)} %gather_fusion.5) | copy-start | bytes 6291460
where the time goes:
time: 873 us; the launch traced here: 865 us
  blocking collectives  259 us (30%)
  local copies, waits for them, and re-layouts  257 us (29%)
  waiting for transfers between devices  214 us (25%)
  matrix products  65.2 us (7%)
  starting transfers between devices  55.3 us (6%)
  other arithmetic  13.4 us (2%)
    all_to_all x1, waiting for transfers between devices, on_device(): lax.all_to_all(back, 'edge', split_axis=0, concat_axis=0, tiled=True)  110 us
    all_to_all x1, blocking collectives, on_device(): lax.all_to_all(send_vals, 'edge', split_axis=0, concat_axis=0, tiled=True)  107 us
    all_to_all x1, waiting for transfers between devices, on_device(): lax.all_to_all(send_vals, 'edge', split_axis=0, concat_axis=0, tiled=True)  104 us
    all_to_all x1, blocking collectives, on_device(): lax.all_to_all(back, 'edge', split_axis=0, concat_axis=0, tiled=True)  101 us
    unnamed x36, local copies, waits for them, and re-layouts  71.2 us
    all_to_all x1, blocking collectives, on_device(): lax.all_to_all(outgoing, 'edge', split_axis=0, concat_axis=0, tiled=True)  51.1 us
    gather x2, local copies, waits for them, and re-layouts, list_sums(): window_rows = jnp.take(padded_rows, window, axis=0)  51.1 us
    gather x2, local copies, waits for them, and re-layouts, list_sums(): window_slots = jnp.take(padded_slots, window, axis=0)  34.4 us
  transfers between devices with their start and end apart: 4, of which 2 were waited for; matrix products, arithmetic and copies ran while one was open for 16% of the time, Pallas kernels for 0%

commit v1 on v0

v1 whole, which is shorter than its diff:
```python
import functools

import jax
import jax.numpy as jnp
from jax import lax
from jax.experimental import pallas as pl
from jax.experimental.pallas import tpu as pltpu
from jax.sharding import PartitionSpec as P

ABLK = 128
BLOCKS = 2
AB_DEV = 2
SIDE = 4
PEERS = SIDE * SIDE * SIDE
STRIDES = (16, 4, 1)
GROUP_AXES = ((0, 1, 2), (1, 2, 0), (2, 0, 1))
GROUP_ROWS = ((0, 176), (176, 176), (352, 160))
MESH = pl.DeviceIdType.MESH
F32 = jnp.float32
BF16 = jnp.bfloat16


def silu(v):
    return v / (1.0 + jnp.exp(-v))


def coords(me):
    return [(me // s) % SIDE for s in STRIDES]


def moved(me, place, axis, step):
    new = (place[axis] + step) % SIDE
    return me + (new - place[axis]) * STRIDES[axis], new


def peer_at(me, i, sign):
    i0, i1, i2 = i % 4, (i // 4) % 4, i // 16
    dx, dz, dy = i0, i1 + i0, i2 + i1 + i0
    px = (me // 16 + sign * dx + 16) % 4
    pz = ((me // 4) % 4 + sign * dz + 16) % 4
    py = (me % 4 + sign * dy + 16) % 4
    return px * 16 + pz * 4 + py


def exchange_kernel(
    layer_block,
    msg,
    w_hbm,
    order,
    places,
    ids,
    paired,
    ids_out,
    weights,
    second,
    outgoing,
    arrived,
    total,
    w_sem,
    send_sem,
    recv_sem,
    id_send,
    id_recv,
):
    me = lax.axis_index("edge")
    rep = lax.axis_index("rep")
    place = coords(me)
    barrier = pltpu.get_barrier_semaphore()

    def greet(i, carry):
        pl.semaphore_signal(barrier, inc=1, device_id=(peer_at(me, i, 1), rep), device_id_type=MESH)
        return carry

    lax.fori_loop(1, PEERS, greet, 0)
    load = pltpu.make_async_copy(w_hbm.at[pl.ds(3 * layer_block, 2)], weights, w_sem)
    load.start()
    load.wait()

    def dense(c, carry):
        rows = pl.ds(pl.multiple_of(c * 256, 256), 256)
        first = silu(jnp.dot(msg[rows, :], weights[0], preferred_element_type=F32)).astype(BF16)
        value = silu(jnp.dot(first, weights[1], preferred_element_type=F32)).astype(BF16)
        second[rows, :] = value
        return carry

    lax.fori_loop(0, 8, dense, 0)
    pl.semaphore_wait(barrier, PEERS - 1)

    id_copies = []
    for axis in range(3):
        ids_out[pl.ds(axis * SIDE + place[axis], 1)] = ids[...][None]
        for step in range(1, SIDE):
            peer, _ = moved(me, place, axis, step)
            copy = pltpu.make_async_remote_copy(
                src_ref=ids,
                dst_ref=ids_out.at[axis * SIDE + place[axis]],
                send_sem=id_send.at[axis * 3 + step - 1],
                recv_sem=id_recv.at[axis * 3 + step - 1],
                device_id=(peer, rep),
                device_id_type=MESH,
            )
            copy.start()
            id_copies.append(copy)

    def message(i):
        return pltpu.make_async_remote_copy(
            src_ref=outgoing.at[pl.ds(pl.multiple_of(i * 32, 32), 32)],
            dst_ref=arrived.at[pl.ds(pl.multiple_of(i * 32, 32), 32)],
            send_sem=send_sem.at[i],
            recv_sem=recv_sem.at[i],
            device_id=(peer_at(me, i, 1), rep),
            device_id_type=MESH,
        )

    def send_chunk(c, carry):
        wanted = jnp.concatenate(
            [
                order[pl.ds(pl.multiple_of(peer_at(me, c * 8 + j, 1) * 32, 32), 32), :]
                for j in range(8)
            ],
            axis=0,
        )
        pick = (wanted == lax.broadcasted_iota(jnp.int32, (256, 2048), 1)).astype(F32).astype(BF16)
        rows = jnp.dot(pick, second[...], preferred_element_type=F32).astype(BF16)
        outgoing[pl.ds(pl.multiple_of(c * 256, 256), 256), :] = rows

        def start(j, inner):
            message(c * 8 + j).start()
            return inner

        @pl.when(c == 0)
        def _():
            arrived[0:32, :] = rows[0:32, :]
            lax.fori_loop(1, 8, start, 0)

        @pl.when(c > 0)
        def _():
            lax.fori_loop(0, 8, start, 0)

        return carry

    lax.fori_loop(0, 8, send_chunk, 0)

    def take_chunk(c, carry):
        def arrive(j, inner):
            @pl.when(c * 8 + j > 0)
            def _():
                message(c * 8 + j).wait_recv()

            return inner

        lax.fori_loop(0, 8, arrive, 0)
        lane = lax.broadcasted_iota(jnp.int32, (1, 256), 1)
        source = peer_at(me, c * 8 + lane // 32, -1) * 32 + lane % 32
        block = arrived[pl.ds(pl.multiple_of(c * 256, 256), 256), :]

        def add(r, inner):
            rows = pl.ds(pl.multiple_of(r * 256, 256), 256)
            pick = (places[rows, :] == source).astype(F32).astype(BF16)
            value = jnp.dot(pick, block, preferred_element_type=F32)

            @pl.when(c == 0)
            def _():
                total[rows, :] = second[rows, :].astype(F32) + value

            @pl.when((c > 0) & (c < 7))
            def _():
                total[rows, :] += value

            @pl.when(c == 7)
            def _():
                paired[rows, :] = (total[rows, :] + value).astype(BF16)

            return inner

        lax.fori_loop(0, 8, add, 0)
        return carry

    lax.fori_loop(0, 8, take_chunk, 0)

    def finish(i, carry):
        message(i).wait_send()
        return carry

    lax.fori_loop(1, PEERS, finish, 0)
    for copy in id_copies:
        copy.wait()


def exchange(layer_block, message, w_edge, order, places, ids):
    rows, feat = message.shape
    vmem = pl.BlockSpec(memory_space=pltpu.VMEM)
    return pl.pallas_call(
        functools.partial(exchange_kernel, layer_block),
        out_shape=(
            jax.ShapeDtypeStruct((rows, feat), BF16),
            jax.ShapeDtypeStruct((3 * SIDE, 8, 128), jnp.int32),
        ),
        in_specs=[vmem, pl.BlockSpec(memory_space=pl.ANY), vmem, vmem, vmem],
        out_specs=(vmem, vmem),
        scratch_shapes=[
            pltpu.VMEM((2, feat, feat), BF16),
            pltpu.VMEM((rows, feat), BF16),
            pltpu.VMEM((rows, feat), BF16),
            pltpu.VMEM((rows, feat), BF16),
            pltpu.VMEM((rows, feat), F32),
            pltpu.SemaphoreType.DMA,
            pltpu.SemaphoreType.DMA((PEERS,)),
            pltpu.SemaphoreType.DMA((PEERS,)),
            pltpu.SemaphoreType.DMA((9,)),
            pltpu.SemaphoreType.DMA((9,)),
        ],
        name=f"exchange{layer_block}",
        compiler_params=pltpu.CompilerParams(collective_id=layer_block, has_side_effects=True),
    )(message, w_edge, order, places, ids)


def sums_kernel(layer_block, list_of, start, stop, pair, w_edge, keys, third, out, acc):
    step = pl.program_id(0)

    @pl.when(step == 0)
    def _():
        def dense(c, carry):
            rows = pl.ds(pl.multiple_of(c * 256, 256), 256)
            value = silu(jnp.dot(pair[rows, :], w_edge[0], preferred_element_type=F32))
            third[rows, :] = value.astype(BF16)
            return carry

        lax.fori_loop(0, 8, dense, 0)

    def one(j, carry):
        which = list_of[step * 8 + j]

        @pl.when(which < 0)
        def _():
            out[j] = jnp.zeros(out.shape[1:], BF16)

        @pl.when(which >= 0)
        def _():
            begin = start[which] // 128
            end = (stop[which] - 1) // 128
            want = which * ABLK + lax.broadcasted_iota(jnp.int32, (ABLK, 128), 0)

            def tile(t):
                pick = (keys[pl.ds(t, 1), :] == want).astype(F32).astype(BF16)
                rows = third[pl.ds(pl.multiple_of(t * 128, 128), 128), :]
                return jnp.dot(pick, rows, preferred_element_type=F32)

            acc[...] = tile(begin)

            def more(t, inner):
                acc[...] += tile(t)
                return inner

            lax.fori_loop(begin + 1, end + 1, more, 0)
            for k in range(4):
                out[j, k * 128 : (k + 1) * 128, :] = acc[:, k * 128 : (k + 1) * 128].astype(BF16)

        return carry

    lax.fori_loop(0, 8, one, 0)


def list_sums(layer_block, pair, w_edge, keys, list_of, start, stop):
    rows, feat = pair.shape
    return pl.pallas_call(
        functools.partial(sums_kernel, layer_block),
        out_shape=(
            jax.ShapeDtypeStruct((rows, feat), BF16),
            jax.ShapeDtypeStruct((PEERS, 512, 128), BF16),
        ),
        grid_spec=pltpu.PrefetchScalarGridSpec(
            num_scalar_prefetch=3,
            grid=(8,),
            in_specs=[
                pl.BlockSpec((rows, feat), lambda i, *_: (0, 0)),
                pl.BlockSpec((1, feat, feat), lambda i, *_: (3 * layer_block + 2, 0, 0)),
                pl.BlockSpec((16, 128), lambda i, *_: (0, 0)),
            ],
            out_specs=[
                pl.BlockSpec((rows, feat), lambda i, *_: (0, 0)),
                pl.BlockSpec((8, 512, 128), lambda i, *_: (i, 0, 0)),
            ],
            scratch_shapes=[pltpu.VMEM((ABLK, feat), F32)],
        ),
        name=f"sums{layer_block}",
        compiler_params=pltpu.CompilerParams(dimension_semantics=("arbitrary",)),
    )(list_of, start, stop, pair, w_edge, keys)


def atoms_kernel(layer_block, bits, sums, w_hbm, atoms, home, atoms_out, *scratch):
    names = ["r1", "t1", "r2", "t2", "r3", "fan", "sel"]
    bufs = {name: scratch[3 * n : 3 * n + 3] for n, name in enumerate(names)}
    flat, weight, w_sem, own_sem, s1, q1, s2, q2, s3, q3, s4, q4, s5, q5, s6, q6, out_sem = scratch[21:]
    me = lax.axis_index("edge")
    rep = lax.axis_index("rep")
    place = coords(me)
    barrier = pltpu.get_barrier_semaphore()
    for axis in range(3):
        for step in range(1, SIDE):
            peer, _ = moved(me, place, axis, step)
            pl.semaphore_signal(barrier, inc=1, device_id=(peer, rep), device_id_type=MESH)
    load = pltpu.make_async_copy(w_hbm.at[layer_block], weight, w_sem)
    load.start()

    def spot(g, va, vb, vc):
        index = [None] * 3
        for axis, value in zip(GROUP_AXES[g], (va, vb, vc)):
            index[axis] = value
        return tuple(index)

    def number(g, va, vb, vc):
        x, z, y = spot(g, va, vb, vc)
        return x * 16 + z * 4 + y

    def rows_of(g):
        return pl.ds(GROUP_ROWS[g][0], GROUP_ROWS[g][1])

    every = pl.ds(0, SIDE)
    send = pltpu.make_async_remote_copy
    here = [[place[axis] for axis in GROUP_AXES[g]] for g in range(3)]
    started = []

    own_copies = {}
    for j in range(SIDE):
        for g in range(3):
            ha, hb, hc = here[g]
            vb = (hb + 1 + j) % SIDE
            copy = pltpu.make_async_copy(
                sums.at[spot(g, ha, vb, every) + (rows_of(g),)], bufs["r1"][g].at[0, j], own_sem.at[g, j]
            )
            copy.start()
            own_copies[g, j] = copy
    pl.semaphore_wait(barrier, 9)

    in1 = {}
    for j in range(SIDE):
        for k in (2, 1, 3):
            for g in range(3):
                ha, hb, hc = here[g]
                peer, va = moved(me, place, GROUP_AXES[g][0], k)
                vb = (hb + 1 + j) % SIDE
                copy = send(
                    src_ref=sums.at[spot(g, va, vb, every) + (rows_of(g),)],
                    dst_ref=bufs["r1"][g].at[k, j],
                    send_sem=s1.at[g, k, j],
                    recv_sem=q1.at[g, k, j],
                    device_id=(peer, rep),
                    device_id_type=MESH,
                )
                copy.start()
                in1[g, k, j] = copy
                started.append(copy)

    in2 = {}
    for j in range(SIDE):
        for g in range(3):
            ha, hb, hc = here[g]
            n = GROUP_ROWS[g][1]
            axis_a = GROUP_AXES[g][0]
            vb = (hb + 1 + j) % SIDE
            own_copies[g, j].wait()
            for k in range(1, SIDE):
                in1[g, k, j].wait_recv()
            r1, t1 = bufs["r1"][g], bufs["t1"][g]

            def one(m, carry, g=g, j=j, ha=ha, hb=hb, hc=hc, vb=vb, axis_a=axis_a, r1=r1, t1=t1, n=n):
                dest = number(g, ha, vb, m)
                low = jnp.zeros((n, 128), F32)
                high = jnp.zeros((n, 128), F32)
                for k in range(SIDE):
                    source = (ha - k + SIDE) % SIDE
                    bit = bits[axis_a * SIDE + source, dest].astype(F32)
                    value = r1[k, j, m].astype(F32)
                    upper = value * bit
                    high = high + upper
                    low = low + (value - upper)
                t1[j, m, 0] = low.astype(BF16)
                t1[j, m, 1] = high.astype(BF16)
                return carry

            lax.fori_loop(0, SIDE, one, 0)
            if j < SIDE - 1:
                peer, _ = moved(me, place, GROUP_AXES[g][1], 1 + j)
                for i in range(SIDE):
                    vc = (hc + 1 + i) % SIDE
                    copy = send(
                        src_ref=t1.at[j, vc],
                        dst_ref=bufs["r2"][g].at[j, vc],
                        send_sem=s2.at[g, j, i],
                        recv_sem=q2.at[g, j, i],
                        device_id=(peer, rep),
                        device_id_type=MESH,
                    )
                    copy.start()
                    in2[g, j, i] = copy
                    started.append(copy)

    in3 = {}
    for i in range(SIDE):
        for g in range(3):
            ha, hb, hc = here[g]
            vc = (hc + 1 + i) % SIDE
            for j in range(SIDE - 1):
                in2[g, j, i].wait_recv()
            t1, r2, t2 = bufs["t1"][g], bufs["r2"][g], bufs["t2"][g]
            for slot in range(AB_DEV):
                value = t1[SIDE - 1, vc, slot].astype(F32)
                for j in range(SIDE - 1):
                    value = value + r2[j, vc, slot].astype(F32)
                t2[i, slot] = value.astype(BF16)
            if i < SIDE - 1:
                peer, _ = moved(me, place, GROUP_AXES[g][2], 1 + i)
                copy = send(
                    src_ref=t2.at[i],
                    dst_ref=bufs["r3"][g].at[i],
                    send_sem=s3.at[g, i],
                    recv_sem=q3.at[g, i],
                    device_id=(peer, rep),
                    device_id_type=MESH,
                )
                copy.start()
                in3[g, i] = copy
                started.append(copy)

    for g in range(3):
        for i in range(SIDE - 1):
            in3[g, i].wait_recv()
        t2, r3 = bufs["t2"][g], bufs["r3"][g]
        for slot in range(AB_DEV):
            value = t2[SIDE - 1, slot].astype(F32)
            for i in range(SIDE - 1):
                value = value + r3[i, slot].astype(F32)
            flat[slot, rows_of(g), :] = value.astype(BF16)

    load.wait()
    for slot in range(AB_DEV):
        gathered = jnp.concatenate([flat[slot, k * 128 : (k + 1) * 128, :] for k in range(4)], axis=1)
        update = silu(jnp.dot(gathered, weight[...], preferred_element_type=F32))
        rows = slice(slot * ABLK, (slot + 1) * ABLK)
        fresh = (atoms[rows, :].astype(F32) + update).astype(BF16)
        atoms_out[rows, :] = fresh
        for k in range(4):
            flat[slot, k * 128 : (k + 1) * 128, :] = fresh[:, k * 128 : (k + 1) * 128]
    in4 = {}
    for g in range(3):
        fan = bufs["fan"][g]
        fan[0, 0] = flat[:, rows_of(g), :]
        for k in (2, 1, 3):
            peer, _ = moved(me, place, GROUP_AXES[g][2], k)
            copy = send(
                src_ref=fan.at[0, 0],
                dst_ref=fan.at[0, k],
                send_sem=s4.at[g, k],
                recv_sem=q4.at[g, k],
                device_id=(peer, rep),
                device_id_type=MESH,
            )
            copy.start()
            in4[g, k] = copy
            started.append(copy)

    in5 = {}
    for i in (0, 1, 3, 2):
        for g in range(3):
            fan = bufs["fan"][g]
            if i:
                in4[g, i].wait_recv()
            for k in (2, 1, 3):
                peer, _ = moved(me, place, GROUP_AXES[g][1], k)
                copy = send(
                    src_ref=fan.at[0, i],
                    dst_ref=fan.at[k, i],
                    send_sem=s5.at[g, k, i],
                    recv_sem=q5.at[g, k, i],
                    device_id=(peer, rep),
                    device_id_type=MESH,
                )
                copy.start()
                in5[g, k, i] = copy
                started.append(copy)

    out_copies = []
    in6 = []
    for j in (0, 1, 3, 2):
        for g in range(3):
            ha, hb, hc = here[g]
            fan, sel = bufs["fan"][g], bufs["sel"][g]
            axis_a = GROUP_AXES[g][0]
            if j:
                for i in range(SIDE):
                    in5[g, j, i].wait_recv()
            vb = (hb - j + SIDE) % SIDE

            def choose(m, carry, g=g, j=j, ha=ha, hc=hc, vb=vb, axis_a=axis_a, fan=fan, sel=sel):
                vc = (hc - m + SIDE) % SIDE
                dest = number(g, ha, vb, vc)
                for k in range(SIDE):
                    bit = bits[axis_a * SIDE + (ha + k) % SIDE, dest]
                    sel[k, j, vc] = jnp.where(bit > 0, fan[j, m, 1], fan[j, m, 0])
                return carry

            lax.fori_loop(0, SIDE, choose, 0)
            target = home.at[spot(g, ha, vb, every) + (rows_of(g),)]
            for k in (2, 1, 3):
                peer, _ = moved(me, place, axis_a, k)
                copy = send(
                    src_ref=sel.at[k, j],
                    dst_ref=target,
                    send_sem=s6.at[g, k, j],
                    recv_sem=q6.at[g, k, j],
                    device_id=(peer, rep),
                    device_id_type=MESH,
                )
                copy.start()
                in6.append(copy)
                started.append(copy)
            copy = pltpu.make_async_copy(sel.at[0, j], target, out_sem.at[g, j])
            copy.start()
            out_copies.append(copy)

    for copy in out_copies:
        copy.wait()
    for copy in in6:
        copy.wait_recv()
    for copy in started:
        copy.wait_send()


def atom_round(layer_block, sums, w_atom, atoms, bits):
    feat = atoms.shape[1]
    vmem = pl.BlockSpec(memory_space=pltpu.VMEM)
    anywhere = pl.BlockSpec(memory_space=pl.ANY)

    def per_group(*lead):
        return [pltpu.VMEM(lead + (n, 128), BF16) for _, n in GROUP_ROWS]

    dma = pltpu.SemaphoreType.DMA
    scratch = (
        per_group(4, 4, 4)
        + per_group(4, 4, 2)
        + per_group(3, 4, 2)
        + per_group(4, 2)
        + per_group(3, 2)
        + per_group(4, 4, 2)
        + per_group(4, 4, 4)
        + [
            pltpu.VMEM((2, 512, 128), BF16),
            pltpu.VMEM((feat, feat), BF16),
            dma,
            dma((3, 4)),
            dma((3, 4, 4)),
            dma((3, 4, 4)),
            dma((3, 3, 4)),
            dma((3, 3, 4)),
            dma((3, 3)),
            dma((3, 3)),
            dma((3, 4)),
            dma((3, 4)),
            dma((3, 4, 4)),
            dma((3, 4, 4)),
            dma((3, 4, 4)),
            dma((3, 4, 4)),
            dma((3, 4)),
        ]
    )
    home, fresh = pl.pallas_call(
        functools.partial(atoms_kernel, layer_block),
        out_shape=(
            jax.ShapeDtypeStruct((SIDE, SIDE, SIDE, 512, 128), BF16),
            jax.ShapeDtypeStruct(atoms.shape, BF16),
        ),
        in_specs=[pl.BlockSpec(memory_space=pltpu.SMEM), anywhere, anywhere, vmem],
        out_specs=(anywhere, vmem),
        scratch_shapes=scratch,
        name=f"atoms{layer_block}",
        compiler_params=pltpu.CompilerParams(
            collective_id=BLOCKS + layer_block, has_side_effects=True, vmem_limit_bytes=56 << 20
        ),
    )(bits, sums.reshape(SIDE, SIDE, SIDE, 512, 128), w_atom, atoms)
    return home.reshape(PEERS, 512, 128), fresh


def fetch_kernel(owner, first, last, msg, third, keys, home, out, blocks, acc, sems):
    count = owner.shape[0]

    def copy(l):
        return pltpu.make_async_copy(home.at[owner[l]], blocks.at[l], sems.at[l])

    def begin(l, carry):
        copy(l).start()
        return carry

    lax.fori_loop(0, count, begin, 0)

    def finish(l, carry):
        copy(l).wait()
        return carry

    lax.fori_loop(0, count, finish, 0)

    def tile(t, carry):
        rows = pl.ds(pl.multiple_of(t * 128, 128), 128)
        acc[...] = msg[rows, :].astype(F32) + third[rows, :].astype(F32)

        def add(l, inner):
            want = l * ABLK + lax.broadcasted_iota(jnp.int32, (128, ABLK), 1)
            pick = (keys[rows, :] == want).astype(F32).astype(BF16)
            block = jnp.concatenate([blocks[l, k * 128 : (k + 1) * 128, :] for k in range(4)], axis=1)
            acc[...] += jnp.dot(pick, block, preferred_element_type=F32)
            return inner

        lax.fori_loop(first[t], last[t] + 1, add, 0)
        out[rows, :] = acc[...].astype(BF16)
        return carry

    lax.fori_loop(0, 16, tile, 0)


def fetch(message, third, keys, home, owner, first, last):
    rows, feat = message.shape
    lists = owner.shape[0]
    vmem = pl.BlockSpec(memory_space=pltpu.VMEM)
    smem = pl.BlockSpec(memory_space=pltpu.SMEM)
    return pl.pallas_call(
        fetch_kernel,
        out_shape=jax.ShapeDtypeStruct((rows, feat), BF16),
        in_specs=[smem, smem, smem, vmem, vmem, vmem, pl.BlockSpec(memory_space=pl.ANY)],
        out_specs=vmem,
        scratch_shapes=[
            pltpu.VMEM((lists, 512, 128), BF16),
            pltpu.VMEM((128, feat), F32),
            pltpu.SemaphoreType.DMA((lists,)),
        ],
        name="fetch",
    )(owner, first, last, message, third, keys, home)


def on_device(
    edge_feats,
    atom_feats,
    w_edge,
    w_atom,
    send_order,
    recv_pos,
    edge_list,
    edge_atom,
    list_block,
    block_home,
):
    lists = list_block.shape[1]
    list_table = jnp.arange(lists, dtype=jnp.int32)
    peer_table = jnp.arange(PEERS, dtype=jnp.int32)
    block_table = jnp.arange(block_home.shape[0], dtype=jnp.int32)
    list_place = jnp.sum(
        jnp.where(list_block[0][:, None] == block_table[None, :], block_home[None, :], 0), axis=1
    )
    owner = list_place // AB_DEV
    placing = owner[None, :] == peer_table[:, None]
    list_of = jnp.max(jnp.where(placing, list_table[None, :], -1), axis=1)
    slot_of = jnp.sum(jnp.where(placing, (list_place % AB_DEV)[None, :], 0), axis=1)
    edge_lists = edge_list[0]
    start = jnp.sum((edge_lists[None, :] < list_table[:, None]).astype(jnp.int32), axis=1)
    stop = jnp.sum((edge_lists[None, :] <= list_table[:, None]).astype(jnp.int32), axis=1)
    tiled_lists = edge_lists.reshape(16, 128)
    first, last = tiled_lists[:, 0], tiled_lists[:, 127]
    keys = edge_lists * ABLK + edge_atom[0]
    keys_row = keys.reshape(16, 128)
    keys_col = keys.reshape(-1, 1)
    order = send_order.reshape(-1, 1)
    places = recv_pos.reshape(-1, 1)
    ids = jnp.broadcast_to(jnp.pad(slot_of, (0, 128 - PEERS))[None, :], (8, 128))
    message, atoms = edge_feats, atom_feats
    for layer_block in range(BLOCKS):
        pair, all_ids = exchange(layer_block, message, w_edge, order, places, ids)
        if layer_block == 0:
            bits = all_ids[:, 0, :]
        third, sums = list_sums(layer_block, pair, w_edge, keys_row, list_of, start, stop)
        home, atoms = atom_round(layer_block, sums, w_atom, atoms, bits)
        message = fetch(message, third, keys_col, home, owner, first, last)
    return message, atoms


def solution(mesh):
    split = P(("rep", "edge"), None)
    whole = P(None, None, None)
    return jax.shard_map(
        on_device,
        mesh=mesh,
        in_specs=(split, split, whole, whole, split, split, split, split, split, P("rep")),
        out_specs=(split, split),
        check_vma=False,
    )
```

time: 873 us -> 415 us (0.48)
  Pallas kernels: 0 us -> 400 us
  blocking collectives: 259 us -> 0 us
  local copies, waits for them, and re-layouts: 257 us -> 9.01 us
  waiting for transfers between devices: 214 us -> 0 us
  matrix products: 65.2 us -> 0 us
  starting transfers between devices: 55.3 us -> 0 us
    pallas_call x0 -> x8, Pallas kernels: none -> 400 us  [the longest x2 228 us: atom_round(): pl.pallas_call(functools.partial(atoms_kernel, layer_block), out_shape=(j...]
    all_to_all x3 -> x0, blocking collectives: 259 us -> none  [the longest x1 107 us: on_device(): lax.all_to_all(send_vals, 'edge', split_axis=0, concat_axis=0, tiled=True)]
    all_to_all x4 -> x0, waiting for transfers between devices: 214 us -> none  [the longest x1 110 us: on_device(): lax.all_to_all(back, 'edge', split_axis=0, concat_axis=0, tiled=True)]
    gather x12 -> x0, local copies, waits for them, and re-layouts: 184 us -> none  [the longest x2 51.1 us: list_sums(): window_rows = jnp.take(padded_rows, window, axis=0)]
    unnamed x36 -> x7, local copies, waits for them, and re-layouts: 71.2 us -> 0.72 us
    dot_general x14 -> x0, matrix products: 65.2 us -> none  [the longest x4 19.8 us: dense_silu(): jnp.dot(values, weight, preferred_element_type=jnp.float32)]
    all_to_all x4 -> x0, starting transfers between devices: 55.3 us -> none  [the longest x1 23 us: on_device(): lax.all_to_all(back, 'edge', split_axis=0, concat_axis=0, tiled=True)]
  transfers between devices with their start and end apart: 4 -> 0, of which waited for: 2 -> 0; matrix products, arithmetic and copies ran while one was open for 16% -> 0% of each run, Pallas kernels for 0% -> 0%
where the time goes in v1:
time: 415 us
  Pallas kernels  400 us (96%)
  local copies, waits for them, and re-layouts  9.01 us (2%)
  other arithmetic  4.88 us (1%)
    pallas_call x2, Pallas kernels, atom_round(): pl.pallas_call(functools.partial(atoms_kernel, layer_block), out_shape=(j...  228 us
    pallas_call x2, Pallas kernels, exchange(): pl.pallas_call(functools.partial(exchange_kernel, layer_block), out_shape...  99.4 us
    pallas_call x2, Pallas kernels, list_sums(): pl.pallas_call(functools.partial(sums_kernel, layer_block), out_shape=(ja...  37.2 us
    pallas_call x2, Pallas kernels, fetch(): pl.pallas_call(fetch_kernel, out_shape=jax.ShapeDtypeStruct((rows, feat),...  35.7 us

profile of v1, /device:TPU:1, one launch (start us, length us, event | category | flops | bytes accessed | tf_op | source)
XLA Modules:
  0.0 414.7 jit_solution(3886540965210078688)
XLA Ops:
  0.6 0.0 copy-start.1
  0.6 0.9 select_reduce_fusion.2
  1.5 0.0 copy-start.2
  1.5 0.6 select_reduce_fusion
  2.1 1.4 convert_reduce_fusion
  3.5 1.5 slice_reduce_fusion
  5.0 0.6 broadcast_in_dim.52.ids
  5.6 1.3 multiply_add_fusion.keys
  6.9 0.7 add_bitcast_fusion
  7.7 1.4 copy.23.keys
  9.0 2.1 copy.20.order
  11.1 0.0 copy-done.1
  11.1 1.4 copy.21.places
  12.4 51.3 %exchange0.1 = (bf16[2048,512]{1,0:T(8,128)(2,1)}, s32[12,8,128]{2,1,0:T(8,128)}) custom-call(bf16[2048,512]{1,0:T(8,128)(2,1)} %msg.3, bf16[6,512,512]{2,1,0:T(8,128)(2,1)} %w_edge.3, s32[2048,1]{1,0:T(8,128)} %copy.20.order, s32[2048,1]{1,0:T(8,128)} %copy.21.places, s32[8,128]{1,0:T(8,128)} %broadcast_in_dim.52.ids), custom_call_target="tpu_custom_call" | custom-call | tf_op jit(solution)/shard_map/exchange0/pallas_call | solution.py:193
  63.8 0.0 copy-done.2
  63.8 0.8 copy.22
  64.6 0.6 slice_bitcast_fusion.bits
  65.2 18.5 %sums0.1 = (bf16[2048,512]{1,0:T(8,128)(2,1)}, bf16[64,512,128]{2,1,0:T(8,128)(2,1)}) custom-call(s32[64]{0:T(128)} %get-tuple-element.29.list_of, s32[32]{0:T(128)} %get-tuple-element.25.start, s32[32]{0:T(128)} %get-tuple-element.24.stop, bf16[2048,512]{1,0:T(8,128)(2,1)} %get-tuple-element.13.pair, bf16[6,512,512]{2,1,0:T(8,128)(2,1)} %w_edge.3, ...), custom_call_target="tpu_custom_call" | custom-call | tf_op jit(solution)/shard_map/sums0/pallas_call | solution.py:266
  83.7 110.4 %atoms0.1 = (bf16[4,4,4,512,128]{4,3,2,1,0:T(8,128)(2,1)}, bf16[256,512]{1,0:T(8,128)(2,1)}) custom-call(s32[12,128]{1,0:T(8,128)} %slice_bitcast_fusion.bits, bf16[4,4,4,512,128]{4,3,2,1,0:T(8,128)(2,1)} %bitcast.17, bf16[2,512,512]{2,1,0:T(8,128)(2,1)} %w_hbm.7, bf16[256,512]{1,0:T(8,128)(2,1)} %atoms.1), custom_call_target="tpu_custom_call" | custom-call | tf_op jit(solution)/shard_map/atoms0/pallas_call | solution.py:567
  194.1 17.8 %fetch.2.msg = bf16[2048,512]{1,0:T(8,128)(2,1)} custom-call(s32[32]{0:T(128)} %copy-done.2, s32[16]{0:T(128)} %get-tuple-element.27.first, s32[16]{0:T(128)} %get-tuple-element.26.last, bf16[2048,512]{1,0:T(8,128)(2,1)} %msg.3, bf16[2048,512]{1,0:T(8,128)(2,1)} %get-tuple-element.14.third, s32[2048,1]{1,0:T(8,128)} %copy.23.keys, bf16[64,512,128]{2,1,0:T(8,128)(2,1)} %bitcast.15), custom_call_target="tpu_custom_call" | custom-call | tf_op jit(solution)/shard_map/fetch/pallas_call | solution.py:625
  212.0 48.1 %exchange1.1 = (bf16[2048,512]{1,0:T(8,128)(2,1)}, s32[12,8,128]{2,1,0:T(8,128)}) custom-call(bf16[2048,512]{1,0:T(8,128)(2,1)} %fetch.2.msg, bf16[6,512,512]{2,1,0:T(8,128)(2,1)} %w_edge.3, s32[2048,1]{1,0:T(8,128)} %copy.20.order, s32[2048,1]{1,0:T(8,128)} %copy.21.places, s32[8,128]{1,0:T(8,128)} %broadcast_in_dim.52.ids), custom_call_target="tpu_custom_call" | custom-call | tf_op jit(solution)/shard_map/exchange1/pallas_call | solution.py:193
  260.1 18.6 %sums1.1 = (bf16[2048,512]{1,0:T(8,128)(2,1)}, bf16[64,512,128]{2,1,0:T(8,128)(2,1)}) custom-call(s32[64]{0:T(128)} %get-tuple-element.29.list_of, s32[32]{0:T(128)} %get-tuple-element.25.start, s32[32]{0:T(128)} %get-tuple-element.24.stop, bf16[2048,512]{1,0:T(8,128)(2,1)} %get-tuple-element.18.pair, bf16[6,512,512]{2,1,0:T(8,128)(2,1)} %w_edge.3, ...), custom_call_target="tpu_custom_call" | custom-call | tf_op jit(solution)/shard_map/sums1/pallas_call | solution.py:266
  278.7 117.4 %atoms1.1 = (bf16[4,4,4,512,128]{4,3,2,1,0:T(8,128)(2,1)}, bf16[256,512]{1,0:T(8,128)(2,1)}) custom-call(s32[12,128]{1,0:T(8,128)} %slice_bitcast_fusion.bits, bf16[4,4,4,512,128]{4,3,2,1,0:T(8,128)(2,1)} %bitcast.16, bf16[2,512,512]{2,1,0:T(8,128)(2,1)} %w_hbm.7, bf16[256,512]{1,0:T(8,128)(2,1)} %get-tuple-element.21.atoms), custom_call_target="tpu_custom_call" | custom-call | tf_op jit(solution)/shard_map/atoms1/pallas_call | solution.py:567
  396.1 0.0 copy-start
  396.1 17.9 %fetch.3 = bf16[2048,512]{1,0:T(8,128)(2,1)} custom-call(s32[32]{0:T(128)} %copy-done.2, s32[16]{0:T(128)} %get-tuple-element.27.first, s32[16]{0:T(128)} %get-tuple-element.26.last, bf16[2048,512]{1,0:T(8,128)(2,1)} %fetch.2.msg, bf16[2048,512]{1,0:T(8,128)(2,1)} %get-tuple-element.19.third, s32[2048,1]{1,0:T(8,128)} %copy.23.keys, ...), custom_call_target="tpu_custom_call" | custom-call | tf_op jit(solution)/shard_map/fetch/pallas_call | solution.py:625
  414.0 0.0 copy-done
  414.0 0.7 copy.28
  (2 shorter events, 0.0 us)
Async XLA Ops:
  0.6 10.4 %copy-start.1 = (s32[1,2048]{1,0:T(1,128)S(1)}, s32[1,2048]{1,0:T(1,128)}, u32[]{:S(2)}) copy-start(s32[1,2048]{1,0:T(1,128)} %param.15) | copy-start | bytes 24580
  1.5 62.2 %copy-start.2 = (s32[32]{0:T(128)}, s32[32]{0:T(128)S(1)}, u32[]{:S(2)}) copy-start(s32[32]{0:T(128)S(1)} %get-tuple-element.31.owner) | copy-start | bytes 388
  396.1 17.9 %copy-start = (bf16[256,512]{1,0:T(8,128)(2,1)S(1)}, bf16[256,512]{1,0:T(8,128)(2,1)}, u32[]{:S(2)}) copy-start(bf16[256,512]{1,0:T(8,128)(2,1)} %get-tuple-element.35) | copy-start | bytes 786436

commit v2 on v1

--- a/solution.py
+++ b/solution.py
@@ -21,7 +21,14 @@
 
 
 def silu(v):
-    return v / (1.0 + jnp.exp(-v))
+    half = 0.5 * v
+    return half + half * jnp.tanh(half)
+
+
+def to_column(rows, column):
+    turned = jnp.transpose(rows[...])
+    for t in range(16):
+        column[t * 128 : (t + 1) * 128, :] = turned[:, t : t + 1]
 
 
 def coords(me):
@@ -46,11 +53,13 @@
     layer_block,
     msg,
     w_hbm,
-    order,
-    places,
+    order_rows,
+    place_rows,
     ids,
     paired,
     ids_out,
+    order,
+    places,
     weights,
     second,
     outgoing,
@@ -72,8 +81,16 @@
         return carry
 
     lax.fori_loop(1, PEERS, greet, 0)
+    if layer_block == 0:
+
+        @pl.when(rep == 1)
+        def _():
+            pl.delay(25000)
+
     load = pltpu.make_async_copy(w_hbm.at[pl.ds(3 * layer_block, 2)], weights, w_sem)
     load.start()
+    to_column(order_rows, order)
+    to_column(place_rows, places)
     load.wait()
 
     def dense(c, carry):
@@ -199,6 +216,8 @@
         in_specs=[vmem, pl.BlockSpec(memory_space=pl.ANY), vmem, vmem, vmem],
         out_specs=(vmem, vmem),
         scratch_shapes=[
+            pltpu.VMEM((rows, 1), jnp.int32),
+            pltpu.VMEM((rows, 1), jnp.int32),
             pltpu.VMEM((2, feat, feat), BF16),
             pltpu.VMEM((rows, feat), BF16),
             pltpu.VMEM((rows, feat), BF16),
@@ -215,77 +234,72 @@
     )(message, w_edge, order, places, ids)
 
 
-def sums_kernel(layer_block, list_of, start, stop, pair, w_edge, keys, third, out, acc):
-    step = pl.program_id(0)
-
-    @pl.when(step == 0)
-    def _():
-        def dense(c, carry):
-            rows = pl.ds(pl.multiple_of(c * 256, 256), 256)
-            value = silu(jnp.dot(pair[rows, :], w_edge[0], preferred_element_type=F32))
-            third[rows, :] = value.astype(BF16)
-            return carry
-
-        lax.fori_loop(0, 8, dense, 0)
-
-    def one(j, carry):
-        which = list_of[step * 8 + j]
-
-        @pl.when(which < 0)
+def sums_kernel(layer_block, list_of, owner, start, pair, w_hbm, keys, third, out, weight, sums, zero, w_sem, sems):
+    load = pltpu.make_async_copy(w_hbm.at[3 * layer_block + 2], weight, w_sem)
+    load.start()
+    zero[...] = jnp.zeros(zero.shape, BF16)
+
+    def clear(d, carry):
+        @pl.when(list_of[d] < 0)
         def _():
-            out[j] = jnp.zeros(out.shape[1:], BF16)
-
-        @pl.when(which >= 0)
-        def _():
-            begin = start[which] // 128
-            end = (stop[which] - 1) // 128
-            want = which * ABLK + lax.broadcasted_iota(jnp.int32, (ABLK, 128), 0)
-
-            def tile(t):
-                pick = (keys[pl.ds(t, 1), :] == want).astype(F32).astype(BF16)
-                rows = third[pl.ds(pl.multiple_of(t * 128, 128), 128), :]
-                return jnp.dot(pick, rows, preferred_element_type=F32)
-
-            acc[...] = tile(begin)
-
-            def more(t, inner):
-                acc[...] += tile(t)
-                return inner
-
-            lax.fori_loop(begin + 1, end + 1, more, 0)
-            for k in range(4):
-                out[j, k * 128 : (k + 1) * 128, :] = acc[:, k * 128 : (k + 1) * 128].astype(BF16)
-
-        return carry
-
-    lax.fori_loop(0, 8, one, 0)
-
-
-def list_sums(layer_block, pair, w_edge, keys, list_of, start, stop):
+            pltpu.make_async_copy(zero, out.at[d], sems.at[d]).start()
+
+        return carry
+
+    lax.fori_loop(0, PEERS, clear, 0)
+    load.wait()
+
+    def dense(c, carry):
+        rows = pl.ds(pl.multiple_of(c * 256, 256), 256)
+        value = silu(jnp.dot(pair[rows, :], weight[...], preferred_element_type=F32))
+        third[rows, :] = value.astype(BF16)
+        return carry
+
+    lax.fori_loop(0, 8, dense, 0)
+
+    def one(l, carry):
+        begin = jnp.minimum(start[l] // 128, 13)
+        key = jnp.concatenate([keys[pl.ds(begin + t, 1), :] for t in range(3)], axis=1)
+        want = l * ABLK + lax.broadcasted_iota(jnp.int32, (ABLK, 384), 0)
+        pick = (key == want).astype(F32).astype(BF16)
+        rows = third[pl.ds(pl.multiple_of(begin * 128, 128), 384), :]
+        value = jnp.dot(pick, rows, preferred_element_type=F32).astype(BF16)
+        for k in range(4):
+            sums[l, k * 128 : (k + 1) * 128, :] = value[:, k * 128 : (k + 1) * 128]
+        pltpu.make_async_copy(sums.at[l], out.at[owner[l]], sems.at[owner[l]]).start()
+        return carry
+
+    lax.fori_loop(0, owner.shape[0], one, 0, unroll=2)
+
+    def finish(d, carry):
+        pltpu.make_async_copy(zero, out.at[d], sems.at[d]).wait()
+        return carry
+
+    lax.fori_loop(0, PEERS, finish, 0)
+
+
+def list_sums(layer_block, pair, w_edge, keys, list_of, owner, start):
     rows, feat = pair.shape
+    vmem = pl.BlockSpec(memory_space=pltpu.VMEM)
+    smem = pl.BlockSpec(memory_space=pltpu.SMEM)
+    anywhere = pl.BlockSpec(memory_space=pl.ANY)
     return pl.pallas_call(
         functools.partial(sums_kernel, layer_block),
         out_shape=(
             jax.ShapeDtypeStruct((rows, feat), BF16),
             jax.ShapeDtypeStruct((PEERS, 512, 128), BF16),
         ),
-        grid_spec=pltpu.PrefetchScalarGridSpec(
-            num_scalar_prefetch=3,
-            grid=(8,),
-            in_specs=[
-                pl.BlockSpec((rows, feat), lambda i, *_: (0, 0)),
-                pl.BlockSpec((1, feat, feat), lambda i, *_: (3 * layer_block + 2, 0, 0)),
-                pl.BlockSpec((16, 128), lambda i, *_: (0, 0)),
-            ],
-            out_specs=[
-                pl.BlockSpec((rows, feat), lambda i, *_: (0, 0)),
-                pl.BlockSpec((8, 512, 128), lambda i, *_: (i, 0, 0)),
-            ],
-            scratch_shapes=[pltpu.VMEM((ABLK, feat), F32)],
-        ),
+        in_specs=[smem, smem, smem, vmem, anywhere, vmem],
+        out_specs=(vmem, anywhere),
+        scratch_shapes=[
+            pltpu.VMEM((feat, feat), BF16),
+            pltpu.VMEM((owner.shape[0], 512, 128), BF16),
+            pltpu.VMEM((512, 128), BF16),
+            pltpu.SemaphoreType.DMA,
+            pltpu.SemaphoreType.DMA((PEERS,)),
+        ],
         name=f"sums{layer_block}",
-        compiler_params=pltpu.CompilerParams(dimension_semantics=("arbitrary",)),
-    )(list_of, start, stop, pair, w_edge, keys)
+    )(list_of, owner, start, pair, w_edge, keys)
 
 
 def atoms_kernel(layer_block, bits, sums, w_hbm, atoms, home, atoms_out, *scratch):
@@ -581,58 +595,94 @@
     return home.reshape(PEERS, 512, 128), fresh
 
 
-def fetch_kernel(owner, first, last, msg, third, keys, home, out, blocks, acc, sems):
+def fetch_kernel(owner, first, last, msg, third, keys, home, out, column, blocks, acc, ready, sems):
     count = owner.shape[0]
+    step = pl.program_id(0)
 
     def copy(l):
         return pltpu.make_async_copy(home.at[owner[l]], blocks.at[l], sems.at[l])
 
-    def begin(l, carry):
-        copy(l).start()
-        return carry
-
-    lax.fori_loop(0, count, begin, 0)
+    @pl.when(step == 0)
+    def _():
+        def begin(l, carry):
+            copy(l).start()
+            return carry
+
+        lax.fori_loop(0, count, begin, 0)
+        ready[0] = 0
+        to_column(keys, column)
 
     def finish(l, carry):
         copy(l).wait()
         return carry
 
-    lax.fori_loop(0, count, finish, 0)
-
-    def tile(t, carry):
-        rows = pl.ds(pl.multiple_of(t * 128, 128), 128)
-        acc[...] = msg[rows, :].astype(F32) + third[rows, :].astype(F32)
-
-        def add(l, inner):
-            want = l * ABLK + lax.broadcasted_iota(jnp.int32, (128, ABLK), 1)
-            pick = (keys[rows, :] == want).astype(F32).astype(BF16)
-            block = jnp.concatenate([blocks[l, k * 128 : (k + 1) * 128, :] for k in range(4)], axis=1)
-            acc[...] += jnp.dot(pick, block, preferred_element_type=F32)
-            return inner
-
-        lax.fori_loop(first[t], last[t] + 1, add, 0)
-        out[rows, :] = acc[...].astype(BF16)
-        return carry
-
-    lax.fori_loop(0, 16, tile, 0)
+    final = step * 4 + 3
+    needed = jnp.where(step == 3, count, jnp.minimum(last[final] + 4, count))
+    lax.fori_loop(ready[0], needed, finish, 0)
+    ready[0] = needed
+
+    for t in range(4):
+        tile = step * 4 + t
+        rows = pl.ds(t * 128, 128)
+        low = first[tile]
+
+        def part(base):
+            want = base * ABLK + lax.broadcasted_iota(jnp.int32, (128, 512), 1)
+            key = column[pl.ds(pl.multiple_of(tile * 128, 128), 128), :]
+            pick = (key == want).astype(F32).astype(BF16)
+            at = [jnp.minimum(base + j, count - 1) for j in range(4)]
+            block = jnp.concatenate(
+                [
+                    jnp.concatenate([blocks[at[j], k * 128 : (k + 1) * 128, :] for k in range(4)], axis=1)
+                    for j in range(4)
+                ],
+                axis=0,
+            )
+            return jnp.dot(pick, block, preferred_element_type=F32)
+
+        base = msg[rows, :].astype(F32) + third[rows, :].astype(F32)
+        found = part(low)
+        out[rows, :] = (base + found).astype(BF16)
+
+        @pl.when(last[tile] >= low + 4)
+        def _():
+            acc[...] = msg[rows, :].astype(F32) + third[rows, :].astype(F32) + part(low)
+
+            def more(i, carry):
+                acc[...] += part(low + 4 * i)
+                return carry
+
+            lax.fori_loop(1, (last[tile] - low) // 4 + 1, more, 0)
+            out[rows, :] = acc[...].astype(BF16)
 
 
 def fetch(message, third, keys, home, owner, first, last):
     rows, feat = message.shape
     lists = owner.shape[0]
-    vmem = pl.BlockSpec(memory_space=pltpu.VMEM)
-    smem = pl.BlockSpec(memory_space=pltpu.SMEM)
+    block = pl.BlockSpec((512, feat), lambda i, *_: (i, 0))
     return pl.pallas_call(
         fetch_kernel,
         out_shape=jax.ShapeDtypeStruct((rows, feat), BF16),
-        in_specs=[smem, smem, smem, vmem, vmem, vmem, pl.BlockSpec(memory_space=pl.ANY)],
-        out_specs=vmem,
-        scratch_shapes=[
-            pltpu.VMEM((lists, 512, 128), BF16),
-            pltpu.VMEM((128, feat), F32),
-            pltpu.SemaphoreType.DMA((lists,)),
-        ],
+        grid_spec=pltpu.PrefetchScalarGridSpec(
+            num_scalar_prefetch=3,
+            grid=(rows // 512,),
+            in_specs=[
+                block,
+                block,
+                pl.BlockSpec((16, 128), lambda i, *_: (0, 0)),
+                pl.BlockSpec(memory_space=pl.ANY),
+            ],
+            out_specs=block,
+            scratch_shapes=[
+                pltpu.VMEM((rows, 1), jnp.int32),
+                pltpu.VMEM((lists, 512, 128), BF16),
+                pltpu.VMEM((128, feat), F32),
+                pltpu.SMEM((1,), jnp.int32),
+                pltpu.SemaphoreType.DMA((lists,)),
+            ],
+        ),
         name="fetch",
+        compiler_params=pltpu.CompilerParams(dimension_semantics=("arbitrary",)),
     )(owner, first, last, message, third, keys, home)
 
 
@@ -661,23 +711,21 @@
     slot_of = jnp.sum(jnp.where(placing, (list_place % AB_DEV)[None, :], 0), axis=1)
     edge_lists = edge_list[0]
     start = jnp.sum((edge_lists[None, :] < list_table[:, None]).astype(jnp.int32), axis=1)
-    stop = jnp.sum((edge_lists[None, :] <= list_table[:, None]).astype(jnp.int32), axis=1)
     tiled_lists = edge_lists.reshape(16, 128)
     first, last = tiled_lists[:, 0], tiled_lists[:, 127]
     keys = edge_lists * ABLK + edge_atom[0]
-    keys_row = keys.reshape(16, 128)
-    keys_col = keys.reshape(-1, 1)
-    order = send_order.reshape(-1, 1)
-    places = recv_pos.reshape(-1, 1)
+    keys = keys.reshape(16, 128)
+    order = send_order.reshape(16, 128)
+    places = recv_pos.reshape(16, 128)
     ids = jnp.broadcast_to(jnp.pad(slot_of, (0, 128 - PEERS))[None, :], (8, 128))
     message, atoms = edge_feats, atom_feats
     for layer_block in range(BLOCKS):
         pair, all_ids = exchange(layer_block, message, w_edge, order, places, ids)
         if layer_block == 0:
             bits = all_ids[:, 0, :]
-        third, sums = list_sums(layer_block, pair, w_edge, keys_row, list_of, start, stop)
+        third, sums = list_sums(layer_block, pair, w_edge, keys, list_of, owner, start)
         home, atoms = atom_round(layer_block, sums, w_atom, atoms, bits)
-        message = fetch(message, third, keys_col, home, owner, first, last)
+        message = fetch(message, third, keys, home, owner, first, last)
     return message, atoms
 
 

time: 415 us -> 351 us (0.85)
  Pallas kernels: 400 us -> 340 us
  local copies, waits for them, and re-layouts: 9.01 us -> 4.24 us
    pallas_call x2, Pallas kernels: 228 us -> 178 us  [atom_round(): pl.pallas_call(functools.partial(atoms_kernel, layer_block), out_shape=(j...]
    pallas_call x2, Pallas kernels: 35.7 us -> 18.5 us  [fetch(): pl.pallas_call(fetch_kernel, out_shape=jax.ShapeDtypeStruct((rows, feat),...]
    pallas_call x2, Pallas kernels: 99.4 us -> 116 us  [exchange(): pl.pallas_call(functools.partial(exchange_kernel, layer_block), out_shape...]
    pallas_call x2, Pallas kernels: 37.2 us -> 26.9 us  [list_sums(): pl.pallas_call(functools.partial(sums_kernel, layer_block), out_shape=(ja...]
where the time goes in v2:
time: 351 us; the launch traced here: 349 us
  Pallas kernels  340 us (97%)
  local copies, waits for them, and re-layouts  4.24 us (1%)
  other arithmetic  4.14 us (1%)
    pallas_call x2, Pallas kernels, atom_round(): pl.pallas_call(functools.partial(atoms_kernel, layer_block), out_shape=(j...  178 us
    pallas_call x2, Pallas kernels, exchange(): pl.pallas_call(functools.partial(exchange_kernel, layer_block), out_shape...  116 us
    pallas_call x2, Pallas kernels, list_sums(): pl.pallas_call(functools.partial(sums_kernel, layer_block), out_shape=(ja...  26.9 us
    pallas_call x2, Pallas kernels, fetch(): pl.pallas_call(fetch_kernel, out_shape=jax.ShapeDtypeStruct((rows, feat),...  18.5 us

profile of v2, /device:TPU:1, one launch (start us, length us, event | category | flops | bytes accessed | tf_op | source)
XLA Modules:
  0.0 348.8 jit_solution(9562028110121439639)
XLA Ops:
  0.6 1.4 convert_reduce_fusion.start
  2.0 0.8 select_reduce_fusion.2
  2.9 0.0 copy-start.1
  2.9 0.6 select_reduce_fusion
  3.5 1.5 slice_reduce_fusion
  5.0 0.6 broadcast_in_dim.51.ids
  5.6 1.3 multiply_add_fusion.keys
  6.9 72.0 %exchange0.1 = (bf16[2048,512]{1,0:T(8,128)(2,1)}, s32[12,8,128]{2,1,0:T(8,128)}) custom-call(bf16[2048,512]{1,0:T(8,128)(2,1)} %msg.3, bf16[6,512,512]{2,1,0:T(8,128)(2,1)} %w_hbm.10, s32[16,128]{1,0:T(8,128)} %bitcast.19, s32[16,128]{1,0:T(8,128)} %bitcast.21, s32[8,128]{1,0:T(8,128)} %broadcast_in_dim.51.ids), custom_call_target="tpu_custom_call" | custom-call | tf_op jit(solution)/shard_map/exchange0/pallas_call | solution.py:210
  78.9 0.0 copy-done.1
  78.9 0.8 copy.14
  79.8 0.6 slice_bitcast_fusion.bits
  80.4 13.4 %sums0.1 = (bf16[2048,512]{1,0:T(8,128)(2,1)}, bf16[64,512,128]{2,1,0:T(8,128)(2,1)}) custom-call(s32[64]{0:T(128)} %get-tuple-element.27.list_of, s32[32]{0:T(128)} %copy-done.1, s32[32]{0:T(128)} %convert_reduce_fusion.start, bf16[2048,512]{1,0:T(8,128)(2,1)} %get-tuple-element.13.pair, bf16[6,512,512]{2,1,0:T(8,128)(2,1)} %w_hbm.10, ...), custom_call_target="tpu_custom_call" | custom-call | tf_op jit(solution)/shard_map/sums0/pallas_call | solution.py:286
  93.8 87.1 %atoms0.1 = (bf16[4,4,4,512,128]{4,3,2,1,0:T(8,128)(2,1)}, bf16[256,512]{1,0:T(8,128)(2,1)}) custom-call(s32[12,128]{1,0:T(8,128)} %slice_bitcast_fusion.bits, bf16[4,4,4,512,128]{4,3,2,1,0:T(8,128)(2,1)} %bitcast.14, bf16[2,512,512]{2,1,0:T(8,128)(2,1)} %w_hbm.11, bf16[256,512]{1,0:T(8,128)(2,1)} %atoms.1), custom_call_target="tpu_custom_call" | custom-call | tf_op jit(solution)/shard_map/atoms0/pallas_call | solution.py:581
  180.9 9.2 %fetch.2.msg = bf16[2048,512]{1,0:T(8,128)(2,1)} custom-call(s32[32]{0:T(128)} %copy-done.1, s32[16]{0:T(128)} %get-tuple-element.25.first, s32[16]{0:T(128)} %get-tuple-element.24.last, bf16[2048,512]{1,0:T(8,128)(2,1)} %msg.3, bf16[2048,512]{1,0:T(8,128)(2,1)} %get-tuple-element.14.third, s32[16,128]{1,0:T(8,128)} %multiply_add_fusion.keys, ...), custom_call_target="tpu_custom_call" | custom-call | tf_op jit(solution)/shard_map/fetch/pallas_call | solution.py:663
  190.1 44.4 %exchange1.1 = (bf16[2048,512]{1,0:T(8,128)(2,1)}, s32[12,8,128]{2,1,0:T(8,128)}) custom-call(bf16[2048,512]{1,0:T(8,128)(2,1)} %fetch.2.msg, bf16[6,512,512]{2,1,0:T(8,128)(2,1)} %w_hbm.10, s32[16,128]{1,0:T(8,128)} %bitcast.20, s32[16,128]{1,0:T(8,128)} %bitcast.22, s32[8,128]{1,0:T(8,128)} %broadcast_in_dim.51.ids), custom_call_target="tpu_custom_call" | custom-call | tf_op jit(solution)/shard_map/exchange1/pallas_call | solution.py:210
  234.5 13.4 %sums1.1 = (bf16[2048,512]{1,0:T(8,128)(2,1)}, bf16[64,512,128]{2,1,0:T(8,128)(2,1)}) custom-call(s32[64]{0:T(128)} %get-tuple-element.27.list_of, s32[32]{0:T(128)} %copy-done.1, s32[32]{0:T(128)} %convert_reduce_fusion.start, bf16[2048,512]{1,0:T(8,128)(2,1)} %get-tuple-element.18.pair, bf16[6,512,512]{2,1,0:T(8,128)(2,1)} %w_hbm.10, ...), custom_call_target="tpu_custom_call" | custom-call | tf_op jit(solution)/shard_map/sums1/pallas_call | solution.py:286
  248.0 90.7 %atoms1.1 = (bf16[4,4,4,512,128]{4,3,2,1,0:T(8,128)(2,1)}, bf16[256,512]{1,0:T(8,128)(2,1)}) custom-call(s32[12,128]{1,0:T(8,128)} %slice_bitcast_fusion.bits, bf16[4,4,4,512,128]{4,3,2,1,0:T(8,128)(2,1)} %bitcast.13, bf16[2,512,512]{2,1,0:T(8,128)(2,1)} %w_hbm.11, bf16[256,512]{1,0:T(8,128)(2,1)} %get-tuple-element.21.atoms), custom_call_target="tpu_custom_call" | custom-call | tf_op jit(solution)/shard_map/atoms1/pallas_call | solution.py:581
  338.7 0.0 copy-start
  338.7 9.3 %fetch.3 = bf16[2048,512]{1,0:T(8,128)(2,1)} custom-call(s32[32]{0:T(128)} %copy-done.1, s32[16]{0:T(128)} %get-tuple-element.25.first, s32[16]{0:T(128)} %get-tuple-element.24.last, bf16[2048,512]{1,0:T(8,128)(2,1)} %fetch.2.msg, bf16[2048,512]{1,0:T(8,128)(2,1)} %get-tuple-element.19.third, s32[16,128]{1,0:T(8,128)} %multiply_add_fusion.keys, ...), custom_call_target="tpu_custom_call" | custom-call | tf_op jit(solution)/shard_map/fetch/pallas_call | solution.py:663
  348.1 0.0 copy-done
  348.1 0.7 copy.16
  (2 shorter events, 0.0 us)
Async XLA Ops:
  2.9 76.1 %copy-start.1 = (s32[32]{0:T(128)}, s32[32]{0:T(128)S(1)}, u32[]{:S(2)}) copy-start(s32[32]{0:T(128)S(1)} %get-tuple-element.29.owner) | copy-start | bytes 388
  338.7 9.3 %copy-start = (bf16[256,512]{1,0:T(8,128)(2,1)S(1)}, bf16[256,512]{1,0:T(8,128)(2,1)}, u32[]{:S(2)}) copy-start(bf16[256,512]{1,0:T(8,128)(2,1)} %get-tuple-element.33) | copy-start | bytes 786436

commit v3 on v2

--- a/solution.py
+++ b/solution.py
@@ -18,6 +18,8 @@
 MESH = pl.DeviceIdType.MESH
 F32 = jnp.float32
 BF16 = jnp.bfloat16
+STAGGER = 25000
+DENSE_ROWS = 256
 
 
 def silu(v):
@@ -53,18 +55,15 @@
     layer_block,
     msg,
     w_hbm,
-    order_rows,
-    place_rows,
+    order,
+    places,
     ids,
     paired,
     ids_out,
-    order,
-    places,
     weights,
-    second,
+    tall,
     outgoing,
     arrived,
-    total,
     w_sem,
     send_sem,
     recv_sem,
@@ -75,6 +74,8 @@
     rep = lax.axis_index("rep")
     place = coords(me)
     barrier = pltpu.get_barrier_semaphore()
+    load = pltpu.make_async_copy(w_hbm.at[pl.ds(3 * layer_block, 2)], weights, w_sem)
+    load.start()
 
     def greet(i, carry):
         pl.semaphore_signal(barrier, inc=1, device_id=(peer_at(me, i, 1), rep), device_id_type=MESH)
@@ -85,22 +86,19 @@
 
         @pl.when(rep == 1)
         def _():
-            pl.delay(25000)
-
-    load = pltpu.make_async_copy(w_hbm.at[pl.ds(3 * layer_block, 2)], weights, w_sem)
-    load.start()
-    to_column(order_rows, order)
-    to_column(place_rows, places)
+            pl.delay(STAGGER)
+
     load.wait()
 
     def dense(c, carry):
-        rows = pl.ds(pl.multiple_of(c * 256, 256), 256)
+        rows = pl.ds(pl.multiple_of(c * DENSE_ROWS, DENSE_ROWS), DENSE_ROWS)
         first = silu(jnp.dot(msg[rows, :], weights[0], preferred_element_type=F32)).astype(BF16)
-        value = silu(jnp.dot(first, weights[1], preferred_element_type=F32)).astype(BF16)
-        second[rows, :] = value
-        return carry
-
-    lax.fori_loop(0, 8, dense, 0)
+        value = silu(jnp.dot(first, weights[1], preferred_element_type=F32)).astype(BF16).astype(F32)
+        for k in range(4):
+            tall[rows, k, :] = value[:, k * 128 : (k + 1) * 128]
+        return carry
+
+    lax.fori_loop(0, msg.shape[0] // DENSE_ROWS, dense, 0)
     pl.semaphore_wait(barrier, PEERS - 1)
 
     id_copies = []
@@ -119,84 +117,50 @@
             copy.start()
             id_copies.append(copy)
 
-    def message(i):
+    def message(i, source):
         return pltpu.make_async_remote_copy(
-            src_ref=outgoing.at[pl.ds(pl.multiple_of(i * 32, 32), 32)],
-            dst_ref=arrived.at[pl.ds(pl.multiple_of(i * 32, 32), 32)],
+            src_ref=outgoing.at[pl.ds(i * 32, 32)],
+            dst_ref=arrived.at[pl.ds(source * 32, 32)],
             send_sem=send_sem.at[i],
             recv_sem=recv_sem.at[i],
             device_id=(peer_at(me, i, 1), rep),
             device_id_type=MESH,
         )
 
-    def send_chunk(c, carry):
-        wanted = jnp.concatenate(
-            [
-                order[pl.ds(pl.multiple_of(peer_at(me, c * 8 + j, 1) * 32, 32), 32), :]
-                for j in range(8)
-            ],
-            axis=0,
-        )
-        pick = (wanted == lax.broadcasted_iota(jnp.int32, (256, 2048), 1)).astype(F32).astype(BF16)
-        rows = jnp.dot(pick, second[...], preferred_element_type=F32).astype(BF16)
-        outgoing[pl.ds(pl.multiple_of(c * 256, 256), 256), :] = rows
-
-        def start(j, inner):
-            message(c * 8 + j).start()
-            return inner
-
-        @pl.when(c == 0)
-        def _():
-            arrived[0:32, :] = rows[0:32, :]
-            lax.fori_loop(1, 8, start, 0)
-
-        @pl.when(c > 0)
-        def _():
-            lax.fori_loop(0, 8, start, 0)
-
-        return carry
-
-    lax.fori_loop(0, 8, send_chunk, 0)
-
-    def take_chunk(c, carry):
-        def arrive(j, inner):
-            @pl.when(c * 8 + j > 0)
-            def _():
-                message(c * 8 + j).wait_recv()
-
-            return inner
-
-        lax.fori_loop(0, 8, arrive, 0)
-        lane = lax.broadcasted_iota(jnp.int32, (1, 256), 1)
-        source = peer_at(me, c * 8 + lane // 32, -1) * 32 + lane % 32
-        block = arrived[pl.ds(pl.multiple_of(c * 256, 256), 256), :]
-
-        def add(r, inner):
-            rows = pl.ds(pl.multiple_of(r * 256, 256), 256)
-            pick = (places[rows, :] == source).astype(F32).astype(BF16)
-            value = jnp.dot(pick, block, preferred_element_type=F32)
-
-            @pl.when(c == 0)
-            def _():
-                total[rows, :] = second[rows, :].astype(F32) + value
-
-            @pl.when((c > 0) & (c < 7))
-            def _():
-                total[rows, :] += value
-
-            @pl.when(c == 7)
-            def _():
-                paired[rows, :] = (total[rows, :] + value).astype(BF16)
-
-            return inner
-
-        lax.fori_loop(0, 8, add, 0)
-        return carry
-
-    lax.fori_loop(0, 8, take_chunk, 0)
+    def row_of(t):
+        return tall[order[t]].astype(BF16)
+
+    for k in range(32):
+        arrived[me * 32 + k] = row_of(me * 32 + k)
+
+    def send_one(i, carry):
+        peer = peer_at(me, i, 1)
+        for k in range(32):
+            outgoing[i * 32 + k] = row_of(peer * 32 + k)
+        message(i, me).start()
+        return carry
+
+    lax.fori_loop(1, PEERS, send_one, 0)
+
+    def arrive(i, carry):
+        message(i, peer_at(me, i, -1)).wait_recv()
+        return carry
+
+    lax.fori_loop(1, PEERS, arrive, 0)
+
+    def add(c, carry):
+        for k in range(32):
+            row = c * 32 + k
+            tall[row] = tall[row] + arrived[places[row]].astype(F32)
+        rows = pl.ds(pl.multiple_of(c * 32, 32), 32)
+        for k in range(4):
+            paired[rows, k * 128 : (k + 1) * 128] = tall[rows, k, :].astype(BF16)
+        return carry
+
+    lax.fori_loop(0, PEERS, add, 0)
 
     def finish(i, carry):
-        message(i).wait_send()
+        message(i, me).wait_send()
         return carry
 
     lax.fori_loop(1, PEERS, finish, 0)
@@ -207,22 +171,20 @@
 def exchange(layer_block, message, w_edge, order, places, ids):
     rows, feat = message.shape
     vmem = pl.BlockSpec(memory_space=pltpu.VMEM)
+    smem = pl.BlockSpec(memory_space=pltpu.SMEM)
     return pl.pallas_call(
         functools.partial(exchange_kernel, layer_block),
         out_shape=(
             jax.ShapeDtypeStruct((rows, feat), BF16),
             jax.ShapeDtypeStruct((3 * SIDE, 8, 128), jnp.int32),
         ),
-        in_specs=[vmem, pl.BlockSpec(memory_space=pl.ANY), vmem, vmem, vmem],
+        in_specs=[vmem, pl.BlockSpec(memory_space=pl.ANY), smem, smem, vmem],
         out_specs=(vmem, vmem),
         scratch_shapes=[
-            pltpu.VMEM((rows, 1), jnp.int32),
-            pltpu.VMEM((rows, 1), jnp.int32),
             pltpu.VMEM((2, feat, feat), BF16),
-            pltpu.VMEM((rows, feat), BF16),
-            pltpu.VMEM((rows, feat), BF16),
-            pltpu.VMEM((rows, feat), BF16),
-            pltpu.VMEM((rows, feat), F32),
+            pltpu.VMEM((rows, 4, 128), F32),
+            pltpu.VMEM((rows, 4, 128), BF16),
+            pltpu.VMEM((rows, 4, 128), BF16),
             pltpu.SemaphoreType.DMA,
             pltpu.SemaphoreType.DMA((PEERS,)),
             pltpu.SemaphoreType.DMA((PEERS,)),
@@ -715,8 +677,8 @@
     first, last = tiled_lists[:, 0], tiled_lists[:, 127]
     keys = edge_lists * ABLK + edge_atom[0]
     keys = keys.reshape(16, 128)
-    order = send_order.reshape(16, 128)
-    places = recv_pos.reshape(16, 128)
+    order = send_order.reshape(-1)
+    places = recv_pos.reshape(-1)
     ids = jnp.broadcast_to(jnp.pad(slot_of, (0, 128 - PEERS))[None, :], (8, 128))
     message, atoms = edge_feats, atom_feats
     for layer_block in range(BLOCKS):

time: 351 us -> 337 us (0.960)
  Pallas kernels: 340 us -> 327 us
    pallas_call x2, Pallas kernels: 116 us -> 101 us  [exchange(): pl.pallas_call(functools.partial(exchange_kernel, layer_block), out_shape...]
where the time goes in v3:
time: 337 us; the launch traced here: 336 us
  Pallas kernels  327 us (97%)
  local copies, waits for them, and re-layouts  4.24 us (1%)
  other arithmetic  4.14 us (1%)
    pallas_call x2, Pallas kernels, atom_round(): pl.pallas_call(functools.partial(atoms_kernel, layer_block), out_shape=(j...  178 us
    pallas_call x2, Pallas kernels, exchange(): pl.pallas_call(functools.partial(exchange_kernel, layer_block), out_shape...  101 us
    pallas_call x2, Pallas kernels, list_sums(): pl.pallas_call(functools.partial(sums_kernel, layer_block), out_shape=(ja...  26.8 us
    pallas_call x2, Pallas kernels, fetch(): pl.pallas_call(fetch_kernel, out_shape=jax.ShapeDtypeStruct((rows, feat),...  20.7 us

profile of v3, /device:TPU:1, one launch (start us, length us, event | category | flops | bytes accessed | tf_op | source)
XLA Modules:
  0.0 336.0 jit_solution(16680802036196691402)
XLA Ops:
  0.6 1.4 convert_reduce_fusion.start
  2.0 0.8 select_reduce_fusion.2
  2.9 0.0 copy-start.1
  2.9 0.6 select_reduce_fusion
  3.5 1.5 slice_reduce_fusion
  5.0 0.6 broadcast_in_dim.51.ids
  5.6 1.3 multiply_add_fusion.keys
  6.9 65.7 %exchange0.1 = (bf16[2048,512]{1,0:T(8,128)(2,1)}, s32[12,8,128]{2,1,0:T(8,128)}) custom-call(bf16[2048,512]{1,0:T(8,128)(2,1)} %msg.3, bf16[6,512,512]{2,1,0:T(8,128)(2,1)} %w_hbm.10, s32[2048]{0:T(1024)} %bitcast.19, s32[2048]{0:T(1024)} %bitcast.21, s32[8,128]{1,0:T(8,128)} %broadcast_in_dim.51.ids), custom_call_target="tpu_custom_call" | custom-call | tf_op jit(solution)/shard_map/exchange0/pallas_call | solution.py:175
  72.6 0.0 copy-done.1
  72.6 0.8 copy.14
  73.4 0.6 slice_bitcast_fusion.bits
  74.0 13.4 %sums0.1 = (bf16[2048,512]{1,0:T(8,128)(2,1)}, bf16[64,512,128]{2,1,0:T(8,128)(2,1)}) custom-call(s32[64]{0:T(128)} %get-tuple-element.27.list_of, s32[32]{0:T(128)} %copy-done.1, s32[32]{0:T(128)} %convert_reduce_fusion.start, bf16[2048,512]{1,0:T(8,128)(2,1)} %get-tuple-element.13.pair, bf16[6,512,512]{2,1,0:T(8,128)(2,1)} %w_hbm.10, ...), custom_call_target="tpu_custom_call" | custom-call | tf_op jit(solution)/shard_map/sums0/pallas_call | solution.py:248
  87.4 87.4 %atoms0.1 = (bf16[4,4,4,512,128]{4,3,2,1,0:T(8,128)(2,1)}, bf16[256,512]{1,0:T(8,128)(2,1)}) custom-call(s32[12,128]{1,0:T(8,128)} %slice_bitcast_fusion.bits, bf16[4,4,4,512,128]{4,3,2,1,0:T(8,128)(2,1)} %bitcast.14, bf16[2,512,512]{2,1,0:T(8,128)(2,1)} %w_hbm.11, bf16[256,512]{1,0:T(8,128)(2,1)} %atoms.1), custom_call_target="tpu_custom_call" | custom-call | tf_op jit(solution)/shard_map/atoms0/pallas_call | solution.py:543
  174.9 10.3 %fetch.2.msg = bf16[2048,512]{1,0:T(8,128)(2,1)} custom-call(s32[32]{0:T(128)} %copy-done.1, s32[16]{0:T(128)} %get-tuple-element.25.first, s32[16]{0:T(128)} %get-tuple-element.24.last, bf16[2048,512]{1,0:T(8,128)(2,1)} %msg.3, bf16[2048,512]{1,0:T(8,128)(2,1)} %get-tuple-element.14.third, s32[16,128]{1,0:T(8,128)} %multiply_add_fusion.keys, ...), custom_call_target="tpu_custom_call" | custom-call | tf_op jit(solution)/shard_map/fetch/pallas_call | solution.py:625
  185.2 35.7 %exchange1.1 = (bf16[2048,512]{1,0:T(8,128)(2,1)}, s32[12,8,128]{2,1,0:T(8,128)}) custom-call(bf16[2048,512]{1,0:T(8,128)(2,1)} %fetch.2.msg, bf16[6,512,512]{2,1,0:T(8,128)(2,1)} %w_hbm.10, s32[2048]{0:T(1024)} %bitcast.20, s32[2048]{0:T(1024)} %bitcast.22, s32[8,128]{1,0:T(8,128)} %broadcast_in_dim.51.ids), custom_call_target="tpu_custom_call" | custom-call | tf_op jit(solution)/shard_map/exchange1/pallas_call | solution.py:175
  220.9 13.4 %sums1.1 = (bf16[2048,512]{1,0:T(8,128)(2,1)}, bf16[64,512,128]{2,1,0:T(8,128)(2,1)}) custom-call(s32[64]{0:T(128)} %get-tuple-element.27.list_of, s32[32]{0:T(128)} %copy-done.1, s32[32]{0:T(128)} %convert_reduce_fusion.start, bf16[2048,512]{1,0:T(8,128)(2,1)} %get-tuple-element.18.pair, bf16[6,512,512]{2,1,0:T(8,128)(2,1)} %w_hbm.10, ...), custom_call_target="tpu_custom_call" | custom-call | tf_op jit(solution)/shard_map/sums1/pallas_call | solution.py:248
  234.3 90.6 %atoms1.1 = (bf16[4,4,4,512,128]{4,3,2,1,0:T(8,128)(2,1)}, bf16[256,512]{1,0:T(8,128)(2,1)}) custom-call(s32[12,128]{1,0:T(8,128)} %slice_bitcast_fusion.bits, bf16[4,4,4,512,128]{4,3,2,1,0:T(8,128)(2,1)} %bitcast.13, bf16[2,512,512]{2,1,0:T(8,128)(2,1)} %w_hbm.11, bf16[256,512]{1,0:T(8,128)(2,1)} %get-tuple-element.21.atoms), custom_call_target="tpu_custom_call" | custom-call | tf_op jit(solution)/shard_map/atoms1/pallas_call | solution.py:543
  324.9 0.0 copy-start
  324.9 10.4 %fetch.3 = bf16[2048,512]{1,0:T(8,128)(2,1)} custom-call(s32[32]{0:T(128)} %copy-done.1, s32[16]{0:T(128)} %get-tuple-element.25.first, s32[16]{0:T(128)} %get-tuple-element.24.last, bf16[2048,512]{1,0:T(8,128)(2,1)} %fetch.2.msg, bf16[2048,512]{1,0:T(8,128)(2,1)} %get-tuple-element.19.third, s32[16,128]{1,0:T(8,128)} %multiply_add_fusion.keys, ...), custom_call_target="tpu_custom_call" | custom-call | tf_op jit(solution)/shard_map/fetch/pallas_call | solution.py:625
  335.3 0.0 copy-done
  335.3 0.7 copy.16
  (2 shorter events, 0.0 us)
Async XLA Ops:
  2.9 69.7 %copy-start.1 = (s32[32]{0:T(128)}, s32[32]{0:T(128)S(1)}, u32[]{:S(2)}) copy-start(s32[32]{0:T(128)S(1)} %get-tuple-element.29.owner) | copy-start | bytes 388
  324.9 10.4 %copy-start = (bf16[256,512]{1,0:T(8,128)(2,1)S(1)}, bf16[256,512]{1,0:T(8,128)(2,1)}, u32[]{:S(2)}) copy-start(bf16[256,512]{1,0:T(8,128)(2,1)} %get-tuple-element.33) | copy-start | bytes 786436

commit v4 on v3

--- a/solution.py
+++ b/solution.py
@@ -18,7 +18,7 @@
 MESH = pl.DeviceIdType.MESH
 F32 = jnp.float32
 BF16 = jnp.bfloat16
-STAGGER = 25000
+STAGGER = 26000
 DENSE_ROWS = 256
 
 
@@ -78,7 +78,9 @@
     load.start()
 
     def greet(i, carry):
-        pl.semaphore_signal(barrier, inc=1, device_id=(peer_at(me, i, 1), rep), device_id_type=MESH)
+        peer = me + i
+        peer = jnp.where(peer >= PEERS, peer - PEERS, peer)
+        pl.semaphore_signal(barrier, inc=1, device_id=(peer, rep), device_id_type=MESH)
         return carry
 
     lax.fori_loop(1, PEERS, greet, 0)
@@ -94,8 +96,7 @@
         rows = pl.ds(pl.multiple_of(c * DENSE_ROWS, DENSE_ROWS), DENSE_ROWS)
         first = silu(jnp.dot(msg[rows, :], weights[0], preferred_element_type=F32)).astype(BF16)
         value = silu(jnp.dot(first, weights[1], preferred_element_type=F32)).astype(BF16).astype(F32)
-        for k in range(4):
-            tall[rows, k, :] = value[:, k * 128 : (k + 1) * 128]
+        tall[rows] = value.reshape(DENSE_ROWS, 4, 128)
         return carry
 
     lax.fori_loop(0, msg.shape[0] // DENSE_ROWS, dense, 0)
@@ -153,8 +154,7 @@
             row = c * 32 + k
             tall[row] = tall[row] + arrived[places[row]].astype(F32)
         rows = pl.ds(pl.multiple_of(c * 32, 32), 32)
-        for k in range(4):
-            paired[rows, k * 128 : (k + 1) * 128] = tall[rows, k, :].astype(BF16)
+        paired[rows, :] = tall[rows].reshape(32, 4 * 128).astype(BF16)
         return carry
 
     lax.fori_loop(0, PEERS, add, 0)

time: 337 us -> 327 us (0.970)
  Pallas kernels: 327 us -> 316 us
    pallas_call x2, Pallas kernels: 101 us -> 91.3 us  [exchange(): pl.pallas_call(functools.partial(exchange_kernel, layer_block), out_shape...]
where the time goes in v4:
time: 327 us; the launch traced here: 326 us
  Pallas kernels  316 us (97%)
  local copies, waits for them, and re-layouts  4.24 us (1%)
  other arithmetic  4.14 us (1%)
    pallas_call x2, Pallas kernels, atom_round(): pl.pallas_call(functools.partial(atoms_kernel, layer_block), out_shape=(j...  177 us
    pallas_call x2, Pallas kernels, exchange(): pl.pallas_call(functools.partial(exchange_kernel, layer_block), out_shape...  91.3 us
    pallas_call x2, Pallas kernels, list_sums(): pl.pallas_call(functools.partial(sums_kernel, layer_block), out_shape=(ja...  26.9 us
    pallas_call x2, Pallas kernels, fetch(): pl.pallas_call(fetch_kernel, out_shape=jax.ShapeDtypeStruct((rows, feat),...  20.8 us

profile of v4, /device:TPU:1, one launch (start us, length us, event | category | flops | bytes accessed | tf_op | source)
XLA Modules:
  0.0 325.5 jit_solution(10379911327077478004)
XLA Ops:
  0.6 1.4 convert_reduce_fusion.start
  2.0 0.8 select_reduce_fusion.2
  2.9 0.0 copy-start.1
  2.9 0.6 select_reduce_fusion
  3.5 1.5 slice_reduce_fusion
  5.0 0.6 broadcast_in_dim.51.ids
  5.6 1.3 multiply_add_fusion.keys
  6.9 60.8 %exchange0.1 = (bf16[2048,512]{1,0:T(8,128)(2,1)}, s32[12,8,128]{2,1,0:T(8,128)}) custom-call(bf16[2048,512]{1,0:T(8,128)(2,1)} %msg.3, bf16[6,512,512]{2,1,0:T(8,128)(2,1)} %w_hbm.10, s32[2048]{0:T(1024)} %bitcast.19, s32[2048]{0:T(1024)} %bitcast.21, s32[8,128]{1,0:T(8,128)} %broadcast_in_dim.51.ids), custom_call_target="tpu_custom_call" | custom-call | tf_op jit(solution)/shard_map/exchange0/pallas_call | solution.py:175
  67.7 0.0 copy-done.1
  67.7 0.8 copy.14
  68.5 0.6 slice_bitcast_fusion.bits
  69.1 13.4 %sums0.1 = (bf16[2048,512]{1,0:T(8,128)(2,1)}, bf16[64,512,128]{2,1,0:T(8,128)(2,1)}) custom-call(s32[64]{0:T(128)} %get-tuple-element.27.list_of, s32[32]{0:T(128)} %copy-done.1, s32[32]{0:T(128)} %convert_reduce_fusion.start, bf16[2048,512]{1,0:T(8,128)(2,1)} %get-tuple-element.13.pair, bf16[6,512,512]{2,1,0:T(8,128)(2,1)} %w_hbm.10, ...), custom_call_target="tpu_custom_call" | custom-call | tf_op jit(solution)/shard_map/sums0/pallas_call | solution.py:248
  82.6 87.0 %atoms0.1 = (bf16[4,4,4,512,128]{4,3,2,1,0:T(8,128)(2,1)}, bf16[256,512]{1,0:T(8,128)(2,1)}) custom-call(s32[12,128]{1,0:T(8,128)} %slice_bitcast_fusion.bits, bf16[4,4,4,512,128]{4,3,2,1,0:T(8,128)(2,1)} %bitcast.14, bf16[2,512,512]{2,1,0:T(8,128)(2,1)} %w_hbm.11, bf16[256,512]{1,0:T(8,128)(2,1)} %atoms.1), custom_call_target="tpu_custom_call" | custom-call | tf_op jit(solution)/shard_map/atoms0/pallas_call | solution.py:543
  169.5 10.4 %fetch.2.msg = bf16[2048,512]{1,0:T(8,128)(2,1)} custom-call(s32[32]{0:T(128)} %copy-done.1, s32[16]{0:T(128)} %get-tuple-element.25.first, s32[16]{0:T(128)} %get-tuple-element.24.last, bf16[2048,512]{1,0:T(8,128)(2,1)} %msg.3, bf16[2048,512]{1,0:T(8,128)(2,1)} %get-tuple-element.14.third, s32[16,128]{1,0:T(8,128)} %multiply_add_fusion.keys, ...), custom_call_target="tpu_custom_call" | custom-call | tf_op jit(solution)/shard_map/fetch/pallas_call | solution.py:625
  179.9 30.5 %exchange1.1 = (bf16[2048,512]{1,0:T(8,128)(2,1)}, s32[12,8,128]{2,1,0:T(8,128)}) custom-call(bf16[2048,512]{1,0:T(8,128)(2,1)} %fetch.2.msg, bf16[6,512,512]{2,1,0:T(8,128)(2,1)} %w_hbm.10, s32[2048]{0:T(1024)} %bitcast.20, s32[2048]{0:T(1024)} %bitcast.22, s32[8,128]{1,0:T(8,128)} %broadcast_in_dim.51.ids), custom_call_target="tpu_custom_call" | custom-call | tf_op jit(solution)/shard_map/exchange1/pallas_call | solution.py:175
  210.4 13.4 %sums1.1 = (bf16[2048,512]{1,0:T(8,128)(2,1)}, bf16[64,512,128]{2,1,0:T(8,128)(2,1)}) custom-call(s32[64]{0:T(128)} %get-tuple-element.27.list_of, s32[32]{0:T(128)} %copy-done.1, s32[32]{0:T(128)} %convert_reduce_fusion.start, bf16[2048,512]{1,0:T(8,128)(2,1)} %get-tuple-element.18.pair, bf16[6,512,512]{2,1,0:T(8,128)(2,1)} %w_hbm.10, ...), custom_call_target="tpu_custom_call" | custom-call | tf_op jit(solution)/shard_map/sums1/pallas_call | solution.py:248
  223.8 90.4 %atoms1.1 = (bf16[4,4,4,512,128]{4,3,2,1,0:T(8,128)(2,1)}, bf16[256,512]{1,0:T(8,128)(2,1)}) custom-call(s32[12,128]{1,0:T(8,128)} %slice_bitcast_fusion.bits, bf16[4,4,4,512,128]{4,3,2,1,0:T(8,128)(2,1)} %bitcast.13, bf16[2,512,512]{2,1,0:T(8,128)(2,1)} %w_hbm.11, bf16[256,512]{1,0:T(8,128)(2,1)} %get-tuple-element.21.atoms), custom_call_target="tpu_custom_call" | custom-call | tf_op jit(solution)/shard_map/atoms1/pallas_call | solution.py:543
  314.3 0.0 copy-start
  314.3 10.5 %fetch.3 = bf16[2048,512]{1,0:T(8,128)(2,1)} custom-call(s32[32]{0:T(128)} %copy-done.1, s32[16]{0:T(128)} %get-tuple-element.25.first, s32[16]{0:T(128)} %get-tuple-element.24.last, bf16[2048,512]{1,0:T(8,128)(2,1)} %fetch.2.msg, bf16[2048,512]{1,0:T(8,128)(2,1)} %get-tuple-element.19.third, s32[16,128]{1,0:T(8,128)} %multiply_add_fusion.keys, ...), custom_call_target="tpu_custom_call" | custom-call | tf_op jit(solution)/shard_map/fetch/pallas_call | solution.py:625
  324.8 0.0 copy-done
  324.8 0.7 copy.16
  (2 shorter events, 0.0 us)
Async XLA Ops:
  2.9 64.9 %copy-start.1 = (s32[32]{0:T(128)}, s32[32]{0:T(128)S(1)}, u32[]{:S(2)}) copy-start(s32[32]{0:T(128)S(1)} %get-tuple-element.29.owner) | copy-start | bytes 388
  314.3 10.5 %copy-start = (bf16[256,512]{1,0:T(8,128)(2,1)S(1)}, bf16[256,512]{1,0:T(8,128)(2,1)}, u32[]{:S(2)}) copy-start(bf16[256,512]{1,0:T(8,128)(2,1)} %get-tuple-element.33) | copy-start | bytes 786436

commit v5 on v4

--- a/solution.py
+++ b/solution.py
@@ -419,53 +419,89 @@
         for k in range(4):
             flat[slot, k * 128 : (k + 1) * 128, :] = fresh[:, k * 128 : (k + 1) * 128]
     in4 = {}
+
+    def hop(g, axis_at, step, source, target, send_sem, recv_sem):
+        peer, _ = moved(me, place, GROUP_AXES[g][axis_at], step)
+        copy = send(
+            src_ref=source,
+            dst_ref=target,
+            send_sem=send_sem,
+            recv_sem=recv_sem,
+            device_id=(peer, rep),
+            device_id_type=MESH,
+        )
+        copy.start()
+        started.append(copy)
+        return copy
+
+    def half(g, which):
+        n = GROUP_ROWS[g][1]
+        cut = (n // 32) * 16 + (n // 16) % 2 * 16
+        return pl.ds(0, cut) if which == 0 else pl.ds(cut, n - cut)
+
+    both = pl.ds(0, AB_DEV)
     for g in range(3):
         fan = bufs["fan"][g]
         fan[0, 0] = flat[:, rows_of(g), :]
-        for k in (2, 1, 3):
-            peer, _ = moved(me, place, GROUP_AXES[g][2], k)
-            copy = send(
-                src_ref=fan.at[0, 0],
-                dst_ref=fan.at[0, k],
-                send_sem=s4.at[g, k],
-                recv_sem=q4.at[g, k],
-                device_id=(peer, rep),
-                device_id_type=MESH,
+        for k in (1, 3):
+            in4[g, k] = hop(g, 2, k, fan.at[0, 0], fan.at[0, k], s4.at[g, k], q4.at[g, k])
+    on4 = {}
+    for g in range(3):
+        fan = bufs["fan"][g]
+        for which, k in enumerate((1, 3)):
+            in4[g, k].wait_recv()
+            rows = half(g, which)
+            on4[g, which] = hop(
+                g,
+                2,
+                k,
+                fan.at[0, k, both, rows],
+                fan.at[0, 2, both, rows],
+                s4.at[g, 2 * which],
+                q4.at[g, 2 * which],
             )
-            copy.start()
-            in4[g, k] = copy
-            started.append(copy)
 
     in5 = {}
     for i in (0, 1, 3, 2):
         for g in range(3):
             fan = bufs["fan"][g]
-            if i:
-                in4[g, i].wait_recv()
-            for k in (2, 1, 3):
-                peer, _ = moved(me, place, GROUP_AXES[g][1], k)
-                copy = send(
-                    src_ref=fan.at[0, i],
-                    dst_ref=fan.at[k, i],
-                    send_sem=s5.at[g, k, i],
-                    recv_sem=q5.at[g, k, i],
-                    device_id=(peer, rep),
-                    device_id_type=MESH,
-                )
-                copy.start()
-                in5[g, k, i] = copy
-                started.append(copy)
+            if i == 2:
+                on4[g, 0].wait_recv()
+                on4[g, 1].wait_recv()
+            for k in (1, 3):
+                in5[g, k, i] = hop(g, 1, k, fan.at[0, i], fan.at[k, i], s5.at[g, k, i], q5.at[g, k, i])
+    on5 = {}
+
+    def forward():
+        for i in (0, 1, 3, 2):
+            for g in range(3):
+                fan = bufs["fan"][g]
+                for which, k in enumerate((1, 3)):
+                    in5[g, k, i].wait_recv()
+                    rows = half(g, which)
+                    on5[g, which, i] = hop(
+                        g,
+                        1,
+                        k,
+                        fan.at[k, i, both, rows],
+                        fan.at[2, i, both, rows],
+                        s5.at[g, 2 * which, i],
+                        q5.at[g, 2 * which, i],
+                    )
 
     out_copies = []
     in6 = []
     for j in (0, 1, 3, 2):
+        if j == 1:
+            forward()
         for g in range(3):
             ha, hb, hc = here[g]
             fan, sel = bufs["fan"][g], bufs["sel"][g]
             axis_a = GROUP_AXES[g][0]
-            if j:
+            if j == 2:
                 for i in range(SIDE):
-                    in5[g, j, i].wait_recv()
+                    on5[g, 0, i].wait_recv()
+                    on5[g, 1, i].wait_recv()
             vb = (hb - j + SIDE) % SIDE
 
             def choose(m, carry, g=g, j=j, ha=ha, hc=hc, vb=vb, axis_a=axis_a, fan=fan, sel=sel):

time: 327 us -> 317 us (0.969)
  Pallas kernels: 316 us -> 307 us
    pallas_call x2, Pallas kernels: 177 us -> 169 us  [atom_round(): pl.pallas_call(functools.partial(atoms_kernel, layer_block), out_shape=(j...]
where the time goes in v5:
time: 317 us; the launch traced here: 316 us
  Pallas kernels  307 us (97%)
  local copies, waits for them, and re-layouts  4.24 us (1%)
  other arithmetic  4.14 us (1%)
    pallas_call x2, Pallas kernels, atom_round(): pl.pallas_call(functools.partial(atoms_kernel, layer_block), out_shape=(j...  169 us
    pallas_call x2, Pallas kernels, exchange(): pl.pallas_call(functools.partial(exchange_kernel, layer_block), out_shape...  91.6 us
    pallas_call x2, Pallas kernels, list_sums(): pl.pallas_call(functools.partial(sums_kernel, layer_block), out_shape=(ja...  26.8 us
    pallas_call x2, Pallas kernels, fetch(): pl.pallas_call(fetch_kernel, out_shape=jax.ShapeDtypeStruct((rows, feat),...  19.7 us

profile of v5, /device:TPU:1, one launch (start us, length us, event | category | flops | bytes accessed | tf_op | source)
XLA Modules:
  0.0 315.8 jit_solution(6251875734715521806)
XLA Ops:
  0.6 1.4 convert_reduce_fusion.start
  2.0 0.8 select_reduce_fusion.2
  2.9 0.0 copy-start.1
  2.9 0.6 select_reduce_fusion
  3.5 1.5 slice_reduce_fusion
  5.0 0.6 broadcast_in_dim.51.ids
  5.6 1.3 multiply_add_fusion.keys
  6.9 60.8 %exchange0.1 = (bf16[2048,512]{1,0:T(8,128)(2,1)}, s32[12,8,128]{2,1,0:T(8,128)}) custom-call(bf16[2048,512]{1,0:T(8,128)(2,1)} %msg.3, bf16[6,512,512]{2,1,0:T(8,128)(2,1)} %w_hbm.10, s32[2048]{0:T(1024)} %bitcast.19, s32[2048]{0:T(1024)} %bitcast.21, s32[8,128]{1,0:T(8,128)} %broadcast_in_dim.51.ids), custom_call_target="tpu_custom_call" | custom-call | tf_op jit(solution)/shard_map/exchange0/pallas_call | solution.py:175
  67.7 0.0 copy-done.1
  67.7 0.8 copy.14
  68.5 0.6 slice_bitcast_fusion.bits
  69.1 13.4 %sums0.1 = (bf16[2048,512]{1,0:T(8,128)(2,1)}, bf16[64,512,128]{2,1,0:T(8,128)(2,1)}) custom-call(s32[64]{0:T(128)} %get-tuple-element.27.list_of, s32[32]{0:T(128)} %copy-done.1, s32[32]{0:T(128)} %convert_reduce_fusion.start, bf16[2048,512]{1,0:T(8,128)(2,1)} %get-tuple-element.13.pair, bf16[6,512,512]{2,1,0:T(8,128)(2,1)} %w_hbm.10, ...), custom_call_target="tpu_custom_call" | custom-call | tf_op jit(solution)/shard_map/sums0/pallas_call | solution.py:248
  82.5 82.5 %atoms0.1 = (bf16[4,4,4,512,128]{4,3,2,1,0:T(8,128)(2,1)}, bf16[256,512]{1,0:T(8,128)(2,1)}) custom-call(s32[12,128]{1,0:T(8,128)} %slice_bitcast_fusion.bits, bf16[4,4,4,512,128]{4,3,2,1,0:T(8,128)(2,1)} %bitcast.14, bf16[2,512,512]{2,1,0:T(8,128)(2,1)} %w_hbm.11, bf16[256,512]{1,0:T(8,128)(2,1)} %atoms.1), custom_call_target="tpu_custom_call" | custom-call | tf_op jit(solution)/shard_map/atoms0/pallas_call | solution.py:579
  165.1 9.8 %fetch.2.msg = bf16[2048,512]{1,0:T(8,128)(2,1)} custom-call(s32[32]{0:T(128)} %copy-done.1, s32[16]{0:T(128)} %get-tuple-element.25.first, s32[16]{0:T(128)} %get-tuple-element.24.last, bf16[2048,512]{1,0:T(8,128)(2,1)} %msg.3, bf16[2048,512]{1,0:T(8,128)(2,1)} %get-tuple-element.14.third, s32[16,128]{1,0:T(8,128)} %multiply_add_fusion.keys, ...), custom_call_target="tpu_custom_call" | custom-call | tf_op jit(solution)/shard_map/fetch/pallas_call | solution.py:661
  174.8 30.9 %exchange1.1 = (bf16[2048,512]{1,0:T(8,128)(2,1)}, s32[12,8,128]{2,1,0:T(8,128)}) custom-call(bf16[2048,512]{1,0:T(8,128)(2,1)} %fetch.2.msg, bf16[6,512,512]{2,1,0:T(8,128)(2,1)} %w_hbm.10, s32[2048]{0:T(1024)} %bitcast.20, s32[2048]{0:T(1024)} %bitcast.22, s32[8,128]{1,0:T(8,128)} %broadcast_in_dim.51.ids), custom_call_target="tpu_custom_call" | custom-call | tf_op jit(solution)/shard_map/exchange1/pallas_call | solution.py:175
  205.7 13.4 %sums1.1 = (bf16[2048,512]{1,0:T(8,128)(2,1)}, bf16[64,512,128]{2,1,0:T(8,128)(2,1)}) custom-call(s32[64]{0:T(128)} %get-tuple-element.27.list_of, s32[32]{0:T(128)} %copy-done.1, s32[32]{0:T(128)} %convert_reduce_fusion.start, bf16[2048,512]{1,0:T(8,128)(2,1)} %get-tuple-element.18.pair, bf16[6,512,512]{2,1,0:T(8,128)(2,1)} %w_hbm.10, ...), custom_call_target="tpu_custom_call" | custom-call | tf_op jit(solution)/shard_map/sums1/pallas_call | solution.py:248
  219.1 86.1 %atoms1.1 = (bf16[4,4,4,512,128]{4,3,2,1,0:T(8,128)(2,1)}, bf16[256,512]{1,0:T(8,128)(2,1)}) custom-call(s32[12,128]{1,0:T(8,128)} %slice_bitcast_fusion.bits, bf16[4,4,4,512,128]{4,3,2,1,0:T(8,128)(2,1)} %bitcast.13, bf16[2,512,512]{2,1,0:T(8,128)(2,1)} %w_hbm.11, bf16[256,512]{1,0:T(8,128)(2,1)} %get-tuple-element.21.atoms), custom_call_target="tpu_custom_call" | custom-call | tf_op jit(solution)/shard_map/atoms1/pallas_call | solution.py:579
  305.2 0.0 copy-start
  305.2 9.9 %fetch.3 = bf16[2048,512]{1,0:T(8,128)(2,1)} custom-call(s32[32]{0:T(128)} %copy-done.1, s32[16]{0:T(128)} %get-tuple-element.25.first, s32[16]{0:T(128)} %get-tuple-element.24.last, bf16[2048,512]{1,0:T(8,128)(2,1)} %fetch.2.msg, bf16[2048,512]{1,0:T(8,128)(2,1)} %get-tuple-element.19.third, s32[16,128]{1,0:T(8,128)} %multiply_add_fusion.keys, ...), custom_call_target="tpu_custom_call" | custom-call | tf_op jit(solution)/shard_map/fetch/pallas_call | solution.py:661
  315.1 0.0 copy-done
  315.1 0.7 copy.16
  (2 shorter events, 0.0 us)
Async XLA Ops:
  2.9 64.9 %copy-start.1 = (s32[32]{0:T(128)}, s32[32]{0:T(128)S(1)}, u32[]{:S(2)}) copy-start(s32[32]{0:T(128)S(1)} %get-tuple-element.29.owner) | copy-start | bytes 388
  305.2 9.9 %copy-start = (bf16[256,512]{1,0:T(8,128)(2,1)S(1)}, bf16[256,512]{1,0:T(8,128)(2,1)}, u32[]{:S(2)}) copy-start(bf16[256,512]{1,0:T(8,128)(2,1)} %get-tuple-element.33) | copy-start | bytes 786436

commit v6 on v5

--- a/solution.py
+++ b/solution.py
@@ -19,7 +19,7 @@
 F32 = jnp.float32
 BF16 = jnp.bfloat16
 STAGGER = 26000
-DENSE_ROWS = 256
+DENSE_ROWS = 512
 
 
 def silu(v):
@@ -212,12 +212,12 @@
     load.wait()
 
     def dense(c, carry):
-        rows = pl.ds(pl.multiple_of(c * 256, 256), 256)
+        rows = pl.ds(pl.multiple_of(c * 512, 512), 512)
         value = silu(jnp.dot(pair[rows, :], weight[...], preferred_element_type=F32))
         third[rows, :] = value.astype(BF16)
         return carry
 
-    lax.fori_loop(0, 8, dense, 0)
+    lax.fori_loop(0, 4, dense, 0)
 
     def one(l, carry):
         begin = jnp.minimum(start[l] // 128, 13)
@@ -231,7 +231,7 @@
         pltpu.make_async_copy(sums.at[l], out.at[owner[l]], sems.at[owner[l]]).start()
         return carry
 
-    lax.fori_loop(0, owner.shape[0], one, 0, unroll=2)
+    lax.fori_loop(0, owner.shape[0], one, 0, unroll=4)
 
     def finish(d, carry):
         pltpu.make_async_copy(zero, out.at[d], sems.at[d]).wait()

time: 317 us -> 310 us (0.978)
  Pallas kernels: 307 us -> 300 us
    pallas_call x2, Pallas kernels: 26.8 us -> 22.5 us  [list_sums(): pl.pallas_call(functools.partial(sums_kernel, layer_block), out_shape=(ja...]
where the time goes in v6:
time: 310 us; the launch traced here: 309 us
  Pallas kernels  300 us (97%)
  local copies, waits for them, and re-layouts  4.24 us (1%)
  other arithmetic  4.14 us (1%)
    pallas_call x2, Pallas kernels, atom_round(): pl.pallas_call(functools.partial(atoms_kernel, layer_block), out_shape=(j...  169 us
    pallas_call x2, Pallas kernels, exchange(): pl.pallas_call(functools.partial(exchange_kernel, layer_block), out_shape...  88.6 us
    pallas_call x2, Pallas kernels, list_sums(): pl.pallas_call(functools.partial(sums_kernel, layer_block), out_shape=(ja...  22.5 us
    pallas_call x2, Pallas kernels, fetch(): pl.pallas_call(fetch_kernel, out_shape=jax.ShapeDtypeStruct((rows, feat),...  19.6 us

profile of v6, /device:TPU:1, one launch (start us, length us, event | category | flops | bytes accessed | tf_op | source)
XLA Modules:
  0.0 309.0 jit_solution(5469249862010483887)
XLA Ops:
  0.6 1.4 convert_reduce_fusion.start
  2.0 0.8 select_reduce_fusion.2
  2.9 0.0 copy-start.1
  2.9 0.6 select_reduce_fusion
  3.5 1.5 slice_reduce_fusion
  5.0 0.6 broadcast_in_dim.51.ids
  5.6 1.3 multiply_add_fusion.keys
  6.9 59.3 %exchange0.1 = (bf16[2048,512]{1,0:T(8,128)(2,1)}, s32[12,8,128]{2,1,0:T(8,128)}) custom-call(bf16[2048,512]{1,0:T(8,128)(2,1)} %msg.3, bf16[6,512,512]{2,1,0:T(8,128)(2,1)} %w_hbm.10, s32[2048]{0:T(1024)} %bitcast.19, s32[2048]{0:T(1024)} %bitcast.21, s32[8,128]{1,0:T(8,128)} %broadcast_in_dim.51.ids), custom_call_target="tpu_custom_call" | custom-call | tf_op jit(solution)/shard_map/exchange0/pallas_call | solution.py:175
  66.2 0.0 copy-done.1
  66.2 0.8 copy.14
  67.0 0.6 slice_bitcast_fusion.bits
  67.6 11.3 %sums0.1 = (bf16[2048,512]{1,0:T(8,128)(2,1)}, bf16[64,512,128]{2,1,0:T(8,128)(2,1)}) custom-call(s32[64]{0:T(128)} %get-tuple-element.27.list_of, s32[32]{0:T(128)} %copy-done.1, s32[32]{0:T(128)} %convert_reduce_fusion.start, bf16[2048,512]{1,0:T(8,128)(2,1)} %get-tuple-element.13.pair, bf16[6,512,512]{2,1,0:T(8,128)(2,1)} %w_hbm.10, ...), custom_call_target="tpu_custom_call" | custom-call | tf_op jit(solution)/shard_map/sums0/pallas_call | solution.py:248
  78.9 82.7 %atoms0.1 = (bf16[4,4,4,512,128]{4,3,2,1,0:T(8,128)(2,1)}, bf16[256,512]{1,0:T(8,128)(2,1)}) custom-call(s32[12,128]{1,0:T(8,128)} %slice_bitcast_fusion.bits, bf16[4,4,4,512,128]{4,3,2,1,0:T(8,128)(2,1)} %bitcast.14, bf16[2,512,512]{2,1,0:T(8,128)(2,1)} %w_hbm.11, bf16[256,512]{1,0:T(8,128)(2,1)} %atoms.1), custom_call_target="tpu_custom_call" | custom-call | tf_op jit(solution)/shard_map/atoms0/pallas_call | solution.py:579
  161.6 9.7 %fetch.2.msg = bf16[2048,512]{1,0:T(8,128)(2,1)} custom-call(s32[32]{0:T(128)} %copy-done.1, s32[16]{0:T(128)} %get-tuple-element.25.first, s32[16]{0:T(128)} %get-tuple-element.24.last, bf16[2048,512]{1,0:T(8,128)(2,1)} %msg.3, bf16[2048,512]{1,0:T(8,128)(2,1)} %get-tuple-element.14.third, s32[16,128]{1,0:T(8,128)} %multiply_add_fusion.keys, ...), custom_call_target="tpu_custom_call" | custom-call | tf_op jit(solution)/shard_map/fetch/pallas_call | solution.py:661
  171.3 29.3 %exchange1.1 = (bf16[2048,512]{1,0:T(8,128)(2,1)}, s32[12,8,128]{2,1,0:T(8,128)}) custom-call(bf16[2048,512]{1,0:T(8,128)(2,1)} %fetch.2.msg, bf16[6,512,512]{2,1,0:T(8,128)(2,1)} %w_hbm.10, s32[2048]{0:T(1024)} %bitcast.20, s32[2048]{0:T(1024)} %bitcast.22, s32[8,128]{1,0:T(8,128)} %broadcast_in_dim.51.ids), custom_call_target="tpu_custom_call" | custom-call | tf_op jit(solution)/shard_map/exchange1/pallas_call | solution.py:175
  200.7 11.2 %sums1.1 = (bf16[2048,512]{1,0:T(8,128)(2,1)}, bf16[64,512,128]{2,1,0:T(8,128)(2,1)}) custom-call(s32[64]{0:T(128)} %get-tuple-element.27.list_of, s32[32]{0:T(128)} %copy-done.1, s32[32]{0:T(128)} %convert_reduce_fusion.start, bf16[2048,512]{1,0:T(8,128)(2,1)} %get-tuple-element.18.pair, bf16[6,512,512]{2,1,0:T(8,128)(2,1)} %w_hbm.10, ...), custom_call_target="tpu_custom_call" | custom-call | tf_op jit(solution)/shard_map/sums1/pallas_call | solution.py:248
  211.9 86.5 %atoms1.1 = (bf16[4,4,4,512,128]{4,3,2,1,0:T(8,128)(2,1)}, bf16[256,512]{1,0:T(8,128)(2,1)}) custom-call(s32[12,128]{1,0:T(8,128)} %slice_bitcast_fusion.bits, bf16[4,4,4,512,128]{4,3,2,1,0:T(8,128)(2,1)} %bitcast.13, bf16[2,512,512]{2,1,0:T(8,128)(2,1)} %w_hbm.11, bf16[256,512]{1,0:T(8,128)(2,1)} %get-tuple-element.21.atoms), custom_call_target="tpu_custom_call" | custom-call | tf_op jit(solution)/shard_map/atoms1/pallas_call | solution.py:579
  298.4 0.0 copy-start
  298.4 9.8 %fetch.3 = bf16[2048,512]{1,0:T(8,128)(2,1)} custom-call(s32[32]{0:T(128)} %copy-done.1, s32[16]{0:T(128)} %get-tuple-element.25.first, s32[16]{0:T(128)} %get-tuple-element.24.last, bf16[2048,512]{1,0:T(8,128)(2,1)} %fetch.2.msg, bf16[2048,512]{1,0:T(8,128)(2,1)} %get-tuple-element.19.third, s32[16,128]{1,0:T(8,128)} %multiply_add_fusion.keys, ...), custom_call_target="tpu_custom_call" | custom-call | tf_op jit(solution)/shard_map/fetch/pallas_call | solution.py:661
  308.3 0.0 copy-done
  308.3 0.7 copy.16
  (2 shorter events, 0.0 us)
Async XLA Ops:
  2.9 63.4 %copy-start.1 = (s32[32]{0:T(128)}, s32[32]{0:T(128)S(1)}, u32[]{:S(2)}) copy-start(s32[32]{0:T(128)S(1)} %get-tuple-element.29.owner) | copy-start | bytes 388
  298.4 9.9 %copy-start = (bf16[256,512]{1,0:T(8,128)(2,1)S(1)}, bf16[256,512]{1,0:T(8,128)(2,1)}, u32[]{:S(2)}) copy-start(bf16[256,512]{1,0:T(8,128)(2,1)} %get-tuple-element.33) | copy-start | bytes 786436

commit v7 on v6

--- a/solution.py
+++ b/solution.py
@@ -18,7 +18,7 @@
 MESH = pl.DeviceIdType.MESH
 F32 = jnp.float32
 BF16 = jnp.bfloat16
-STAGGER = 26000
+STAGGER = 25000
 DENSE_ROWS = 512
 
 
@@ -157,7 +157,7 @@
         paired[rows, :] = tall[rows].reshape(32, 4 * 128).astype(BF16)
         return carry
 
-    lax.fori_loop(0, PEERS, add, 0)
+    lax.fori_loop(0, PEERS, add, 0, unroll=2)
 
     def finish(i, carry):
         message(i, me).wait_send()
@@ -212,12 +212,12 @@
     load.wait()
 
     def dense(c, carry):
-        rows = pl.ds(pl.multiple_of(c * 512, 512), 512)
+        rows = pl.ds(pl.multiple_of(c * 1024, 1024), 1024)
         value = silu(jnp.dot(pair[rows, :], weight[...], preferred_element_type=F32))
         third[rows, :] = value.astype(BF16)
         return carry
 
-    lax.fori_loop(0, 4, dense, 0)
+    lax.fori_loop(0, 2, dense, 0)
 
     def one(l, carry):
         begin = jnp.minimum(start[l] // 128, 13)
@@ -231,7 +231,7 @@
         pltpu.make_async_copy(sums.at[l], out.at[owner[l]], sems.at[owner[l]]).start()
         return carry
 
-    lax.fori_loop(0, owner.shape[0], one, 0, unroll=4)
+    lax.fori_loop(0, owner.shape[0], one, 0, unroll=8)
 
     def finish(d, carry):
         pltpu.make_async_copy(zero, out.at[d], sems.at[d]).wait()

time: 310 us -> 309 us (level)
  no operation moved by 1% of the time
where the time goes in v7:
time: 309 us; the launch traced here: 307 us
  Pallas kernels  298 us (96%)
  local copies, waits for them, and re-layouts  4.24 us (1%)
  other arithmetic  4.14 us (1%)
    pallas_call x2, Pallas kernels, atom_round(): pl.pallas_call(functools.partial(atoms_kernel, layer_block), out_shape=(j...  170 us
    pallas_call x2, Pallas kernels, exchange(): pl.pallas_call(functools.partial(exchange_kernel, layer_block), out_shape...  87.8 us
    pallas_call x2, Pallas kernels, list_sums(): pl.pallas_call(functools.partial(sums_kernel, layer_block), out_shape=(ja...  20.9 us
    pallas_call x2, Pallas kernels, fetch(): pl.pallas_call(fetch_kernel, out_shape=jax.ShapeDtypeStruct((rows, feat),...  18.6 us

profile of v7, /device:TPU:1, one launch (start us, length us, event | category | flops | bytes accessed | tf_op | source)
XLA Modules:
  0.0 306.8 jit_solution(6724038920687870592)
XLA Ops:
  0.6 1.4 convert_reduce_fusion.start
  2.0 0.8 select_reduce_fusion.2
  2.9 0.0 copy-start.1
  2.9 0.6 select_reduce_fusion
  3.5 1.5 slice_reduce_fusion
  5.0 0.6 broadcast_in_dim.51.ids
  5.6 1.3 multiply_add_fusion.keys
  6.9 58.0 %exchange0.1 = (bf16[2048,512]{1,0:T(8,128)(2,1)}, s32[12,8,128]{2,1,0:T(8,128)}) custom-call(bf16[2048,512]{1,0:T(8,128)(2,1)} %msg.3, bf16[6,512,512]{2,1,0:T(8,128)(2,1)} %w_hbm.10, s32[2048]{0:T(1024)} %bitcast.19, s32[2048]{0:T(1024)} %bitcast.21, s32[8,128]{1,0:T(8,128)} %broadcast_in_dim.51.ids), custom_call_target="tpu_custom_call" | custom-call | tf_op jit(solution)/shard_map/exchange0/pallas_call | solution.py:175
  64.9 0.0 copy-done.1
  64.9 0.8 copy.14
  65.7 0.6 slice_bitcast_fusion.bits
  66.3 10.4 %sums0.1 = (bf16[2048,512]{1,0:T(8,128)(2,1)}, bf16[64,512,128]{2,1,0:T(8,128)(2,1)}) custom-call(s32[64]{0:T(128)} %get-tuple-element.27.list_of, s32[32]{0:T(128)} %copy-done.1, s32[32]{0:T(128)} %convert_reduce_fusion.start, bf16[2048,512]{1,0:T(8,128)(2,1)} %get-tuple-element.13.pair, bf16[6,512,512]{2,1,0:T(8,128)(2,1)} %w_hbm.10, ...), custom_call_target="tpu_custom_call" | custom-call | tf_op jit(solution)/shard_map/sums0/pallas_call | solution.py:248
  76.7 83.4 %atoms0.1 = (bf16[4,4,4,512,128]{4,3,2,1,0:T(8,128)(2,1)}, bf16[256,512]{1,0:T(8,128)(2,1)}) custom-call(s32[12,128]{1,0:T(8,128)} %slice_bitcast_fusion.bits, bf16[4,4,4,512,128]{4,3,2,1,0:T(8,128)(2,1)} %bitcast.14, bf16[2,512,512]{2,1,0:T(8,128)(2,1)} %w_hbm.11, bf16[256,512]{1,0:T(8,128)(2,1)} %atoms.1), custom_call_target="tpu_custom_call" | custom-call | tf_op jit(solution)/shard_map/atoms0/pallas_call | solution.py:579
  160.1 9.2 %fetch.2.msg = bf16[2048,512]{1,0:T(8,128)(2,1)} custom-call(s32[32]{0:T(128)} %copy-done.1, s32[16]{0:T(128)} %get-tuple-element.25.first, s32[16]{0:T(128)} %get-tuple-element.24.last, bf16[2048,512]{1,0:T(8,128)(2,1)} %msg.3, bf16[2048,512]{1,0:T(8,128)(2,1)} %get-tuple-element.14.third, s32[16,128]{1,0:T(8,128)} %multiply_add_fusion.keys, ...), custom_call_target="tpu_custom_call" | custom-call | tf_op jit(solution)/shard_map/fetch/pallas_call | solution.py:661
  169.4 29.8 %exchange1.1 = (bf16[2048,512]{1,0:T(8,128)(2,1)}, s32[12,8,128]{2,1,0:T(8,128)}) custom-call(bf16[2048,512]{1,0:T(8,128)(2,1)} %fetch.2.msg, bf16[6,512,512]{2,1,0:T(8,128)(2,1)} %w_hbm.10, s32[2048]{0:T(1024)} %bitcast.20, s32[2048]{0:T(1024)} %bitcast.22, s32[8,128]{1,0:T(8,128)} %broadcast_in_dim.51.ids), custom_call_target="tpu_custom_call" | custom-call | tf_op jit(solution)/shard_map/exchange1/pallas_call | solution.py:175
  199.2 10.5 %sums1.1 = (bf16[2048,512]{1,0:T(8,128)(2,1)}, bf16[64,512,128]{2,1,0:T(8,128)(2,1)}) custom-call(s32[64]{0:T(128)} %get-tuple-element.27.list_of, s32[32]{0:T(128)} %copy-done.1, s32[32]{0:T(128)} %convert_reduce_fusion.start, bf16[2048,512]{1,0:T(8,128)(2,1)} %get-tuple-element.18.pair, bf16[6,512,512]{2,1,0:T(8,128)(2,1)} %w_hbm.10, ...), custom_call_target="tpu_custom_call" | custom-call | tf_op jit(solution)/shard_map/sums1/pallas_call | solution.py:248
  209.7 87.0 %atoms1.1 = (bf16[4,4,4,512,128]{4,3,2,1,0:T(8,128)(2,1)}, bf16[256,512]{1,0:T(8,128)(2,1)}) custom-call(s32[12,128]{1,0:T(8,128)} %slice_bitcast_fusion.bits, bf16[4,4,4,512,128]{4,3,2,1,0:T(8,128)(2,1)} %bitcast.13, bf16[2,512,512]{2,1,0:T(8,128)(2,1)} %w_hbm.11, bf16[256,512]{1,0:T(8,128)(2,1)} %get-tuple-element.21.atoms), custom_call_target="tpu_custom_call" | custom-call | tf_op jit(solution)/shard_map/atoms1/pallas_call | solution.py:579
  296.7 0.0 copy-start
  296.7 9.3 %fetch.3 = bf16[2048,512]{1,0:T(8,128)(2,1)} custom-call(s32[32]{0:T(128)} %copy-done.1, s32[16]{0:T(128)} %get-tuple-element.25.first, s32[16]{0:T(128)} %get-tuple-element.24.last, bf16[2048,512]{1,0:T(8,128)(2,1)} %fetch.2.msg, bf16[2048,512]{1,0:T(8,128)(2,1)} %get-tuple-element.19.third, s32[16,128]{1,0:T(8,128)} %multiply_add_fusion.keys, ...), custom_call_target="tpu_custom_call" | custom-call | tf_op jit(solution)/shard_map/fetch/pallas_call | solution.py:661
  306.1 0.0 copy-done
  306.1 0.7 copy.16
  (2 shorter events, 0.0 us)
Async XLA Ops:
  2.9 62.0 %copy-start.1 = (s32[32]{0:T(128)}, s32[32]{0:T(128)S(1)}, u32[]{:S(2)}) copy-start(s32[32]{0:T(128)S(1)} %get-tuple-element.29.owner) | copy-start | bytes 388
  296.7 9.4 %copy-start = (bf16[256,512]{1,0:T(8,128)(2,1)S(1)}, bf16[256,512]{1,0:T(8,128)(2,1)}, u32[]{:S(2)}) copy-start(bf16[256,512]{1,0:T(8,128)(2,1)} %get-tuple-element.33) | copy-start | bytes 786436
